TPU v7x, 128 devices: a whole 4x4x4 slice. The times are simulated.
128 devices in a mesh: scan: 32 (over z, x, core), col: 4 (over y).
Axes of the slice: x: 4, y: 4, z: 4, core: 2. Of those that a mesh axis runs over, the one named last changes fastest.
Arguments:
- object_field: float32 [2, 8192, 1024], P(None, 'scan', 'col'), may hold values from -6 to 6
- amplitudes: bfloat16 [256, 256, 256], P(('scan', 'col')), may hold values from 0.099609375 to 3
- positions: int32 [256, 2], P(('scan', 'col')), may hold values from 0 to 7936, as said below
- frame_count: int32 [128], P(('scan', 'col')), may hold values from 1 to 2, as said below
- coefficients: float32 [256, 4], P(('scan', 'col')), may hold values from -6 to 6
- probe_modes: float32 [4, 2, 256, 256], replicated, may hold values from -6 to 6
Outputs:
- refined_object: float32 [2, 8192, 1024], P(None, 'scan', 'col')
- refined_modes: float32 [4, 2, 256, 256], replicated
- refined_coefficients: float32 [256, 4], P(('scan', 'col'))
Inputs may be any that keep to these rules, and one draw needn't show every extreme that they name: `positions`: frame g belongs to the device of index g // 2 along scan+col (scan slowest). Its top-left pixel lies in that device's block of 256 x 256 pixels, and its 256 x 256 patch lies inside the object. Entry d counts the live frames of the device of index d along scan+col: its first frame_count[d] slots are live, the rest are ignored. Some device has 2.
All inputs are finite; a program needn't handle non-finite values.
Results may differ from a plain program's by a relative error of at most 0.0058.
Values sent between devices are 32-bit elements; how exact they have to be, the bound alone decides.
No kernel may reach another device: no remote copies, remote signals or barrier semaphores. Data moves between devices by JAX's collectives and lax.ppermute only.
A program may use at most 128 MiB of HBM per device.

v0:
```python
import functools
import math

import jax
import jax.numpy as jnp
import numpy as np
from jax import lax
from jax.experimental import pallas as pl
from jax.experimental.pallas import tpu as pltpu
from jax.sharding import Mesh
from jax.sharding import PartitionSpec as P

ITERS = 2
F32 = jnp.float32
BF16 = jnp.bfloat16
CHIPS = ("z", "x", "y")
SCAN = ("z", "x", "core")
ALL = ("z", "x", "core", "y")
ROWS = 32


def make_tables(length):
    indices = jnp.arange(length, dtype=jnp.int32)
    phases = indices[:, None] * indices[None, :] % length
    angles = phases.astype(F32) * (2.0 * math.pi / length)
    factor = 1.0 / math.sqrt(length)
    cosine = (jnp.cos(angles) * factor).astype(BF16)
    sine = (jnp.sin(angles) * factor).astype(BF16)
    return cosine, sine


def fill_tables(cos_ref, sin_ref, rows_ref, cols_ref):
    n = cos_ref.shape[0]
    cosine = cos_ref[...]
    sine = sin_ref[...]
    rows_ref[:n, :n] = cosine
    rows_ref[:n, n:] = sine
    rows_ref[n:, :n] = -sine
    rows_ref[n:, n:] = cosine
    cols_ref[:n, :n] = cosine
    cols_ref[:n, n:] = -sine
    cols_ref[n:, :n] = sine
    cols_ref[n:, n:] = cosine


def frames_kernel(
    core_ref, pos_ref, cnt_ref, coef_ref, own_ref, right_ref, below_ref, corner_ref,
    amp_ref, modes_ref, cos_ref, sin_ref,
    keep_ref, give_ref, grads_ref, t_own_ref, t_right_ref, t_below_ref, t_corner_ref,
    ext_ref, tot_ref, probe_ref, exit_ref, rows_ref, cols_ref, stack_ref, side_ref, wide_ref,
    in_sem, out_sem,
):
    frames, n = amp_ref.shape[0], amp_ref.shape[1]
    modes = modes_ref.shape[0]
    loads = []
    for i, (src, a, b) in enumerate(
        ((own_ref, 0, 0), (right_ref, 0, n), (below_ref, n, 0), (corner_ref, n, n))
    ):
        loads.append(pltpu.make_async_copy(src, ext_ref.at[:, a : a + n, b : b + n], in_sem.at[i]))
    for load in loads:
        load.start()
    fill_tables(cos_ref, sin_ref, rows_ref, cols_ref)
    tot_ref[...] = jnp.zeros_like(tot_ref)
    is_first = core_ref[0] == 0
    offsets = [(pos_ref[f, 0] & (n - 1), pos_ref[f, 1] & (n - 1)) for f in range(frames)]
    weights = [
        [jnp.where(f < cnt_ref[0], coef_ref[f, k], 0.0) for k in range(modes)] for f in range(frames)
    ]
    for load in loads:
        load.wait()

    def patch_rows(f, plane, b):
        r, c = offsets[f]
        base = pl.multiple_of((r >> 3) * 8 + b * ROWS, 8)
        rows = ext_ref[plane, pl.ds(base, ROWS + 8), :]
        rows = pltpu.roll(rows, (2 * n - c) & (2 * n - 1), 1)[:, :n]
        return pltpu.roll(rows, ROWS + 8 - (r & 7), 0)[:ROWS]

    def start(b, carry):
        at = pl.ds(pl.multiple_of(b * ROWS, ROWS), ROWS)
        at_imag = pl.ds(pl.multiple_of(n + b * ROWS, ROWS), ROWS)
        for f in range(frames):
            o_re = patch_rows(f, 0, b)
            o_im = patch_rows(f, 1, b)
            grads_ref[f, 0, at, :] = o_re
            grads_ref[f, 1, at, :] = o_im
            p_re = weights[f][0] * modes_ref[0, 0, at, :]
            p_im = weights[f][0] * modes_ref[0, 1, at, :]
            for k in range(1, modes):
                p_re = p_re + weights[f][k] * modes_ref[k, 0, at, :]
                p_im = p_im + weights[f][k] * modes_ref[k, 1, at, :]
            probe_ref[f, 0, at, :] = p_re
            probe_ref[f, 1, at, :] = p_im
            e_re = p_re * o_re - p_im * o_im
            e_im = p_re * o_im + p_im * o_re
            exit_ref[f, 0, at, :] = e_re
            exit_ref[f, 1, at, :] = e_im
            stack_ref[at, f * n : (f + 1) * n] = e_re.astype(BF16)
            stack_ref[at_imag, f * n : (f + 1) * n] = e_im.astype(BF16)
        return carry

    lax.fori_loop(0, n // ROWS, start, 0)

    def transform(first_ref, second_ref):
        for f in range(frames):
            cols = slice(f * n, (f + 1) * n)
            for h in range(2):
                half = jnp.dot(
                    first_ref[h * n : (h + 1) * n, :], stack_ref[:, cols], preferred_element_type=F32
                )
                side_ref[cols, h * n : (h + 1) * n] = half.astype(BF16)
        for f in range(frames):
            cols = slice(f * n, (f + 1) * n)
            wide_ref[cols, :] = jnp.dot(side_ref[cols, :], second_ref[...], preferred_element_type=F32)

    transform(rows_ref, cols_ref)

    def scale(b, carry):
        at = pl.ds(pl.multiple_of(b * ROWS, ROWS), ROWS)
        at_imag = pl.ds(pl.multiple_of(n + b * ROWS, ROWS), ROWS)
        for f in range(frames):
            at_f = pl.ds(pl.multiple_of(f * n + b * ROWS, ROWS), ROWS)
            far_re = wide_ref[at_f, :n]
            far_im = wide_ref[at_f, n:]
            inverse = jnp.minimum(lax.rsqrt(far_re * far_re + far_im * far_im), 2.0)
            factor = amp_ref[f, at, :].astype(F32) * inverse
            stack_ref[at, f * n : (f + 1) * n] = (far_re * factor).astype(BF16)
            stack_ref[at_imag, f * n : (f + 1) * n] = (far_im * factor).astype(BF16)
        return carry

    lax.fori_loop(0, n // ROWS, scale, 0)
    transform(cols_ref, rows_ref)

    def finish(b, carry):
        at = pl.ds(pl.multiple_of(b * ROWS, ROWS), ROWS)
        sums = [[None, None] for _ in range(modes)]
        pad = jnp.zeros((8, n), F32)
        beside = jnp.zeros((ROWS + 8, n), F32)
        for f in range(frames):
            r, c = offsets[f]
            at_f = pl.ds(pl.multiple_of(f * n + b * ROWS, ROWS), ROWS)
            d_re = wide_ref[at_f, :n] - exit_ref[f, 0, at, :]
            d_im = wide_ref[at_f, n:] - exit_ref[f, 1, at, :]
            p_re = probe_ref[f, 0, at, :]
            p_im = probe_ref[f, 1, at, :]
            updates = (
                p_re * d_re + p_im * d_im,
                p_re * d_im - p_im * d_re,
                p_re * p_re + p_im * p_im,
            )
            for q in range(3):
                placed = pltpu.roll(jnp.concatenate([updates[q], pad], 0), r & 7, 0)
                placed = pltpu.roll(jnp.concatenate([placed, beside], 1), c, 1)
                rows = pl.ds(pl.multiple_of((r >> 3) * 8 + b * ROWS, 8), ROWS + 8)
                tot_ref[q, rows, :] = tot_ref[q, rows, :] + placed
            o_re = grads_ref[f, 0, at, :]
            o_im = grads_ref[f, 1, at, :]
            g_re = o_re * d_re + o_im * d_im
            g_im = o_re * d_im - o_im * d_re
            grads_ref[f, 0, at, :] = g_re
            grads_ref[f, 1, at, :] = g_im
            for k in range(modes):
                for q, g in ((0, g_re), (1, g_im)):
                    term = weights[f][k] * g
                    sums[k][q] = term if f == 0 else sums[k][q] + term
        for k in range(modes):
            keep = jnp.where(is_first, sums[k][0], sums[k][1])
            give = jnp.where(is_first, sums[k][1], sums[k][0])
            for i in range(ROWS // 8):
                for j in range(n // 128):
                    tile = b * (ROWS // 8 * (n // 128)) + i * (n // 128) + j
                    keep_ref[tile, k] = keep[8 * i : 8 * i + 8, 128 * j : 128 * j + 128]
                    give_ref[tile, k] = give[8 * i : 8 * i + 8, 128 * j : 128 * j + 128]
        return carry

    lax.fori_loop(0, n // ROWS, finish, 0)
    stores = []
    for i, (dst, a, b) in enumerate(
        ((t_own_ref, 0, 0), (t_right_ref, 0, n), (t_below_ref, n, 0), (t_corner_ref, n, n))
    ):
        stores.append(pltpu.make_async_copy(tot_ref.at[:, a : a + n, b : b + n], dst, out_sem.at[i]))
    for store in stores:
        store.start()
    for store in stores:
        store.wait()


def run_frames(core, positions, count, coefficients, blocks, amplitudes, modes, tables):
    frames, n = amplitudes.shape[0], amplitudes.shape[1]
    k = modes.shape[0]
    tiles = n * n // 1024
    smem = pl.BlockSpec(memory_space=pltpu.SMEM)
    vmem = pl.BlockSpec(memory_space=pltpu.VMEM)
    hbm = pl.BlockSpec(memory_space=pl.ANY)
    piece = jax.ShapeDtypeStruct((tiles, k, 8, 128), F32)
    quarter = jax.ShapeDtypeStruct((3, n, n), F32)
    return pl.pallas_call(
        frames_kernel,
        out_shape=(piece, piece, jax.ShapeDtypeStruct((frames, 2, n, n), F32)) + (quarter,) * 4,
        in_specs=[smem] * 4 + [hbm] * 4 + [vmem] * 4,
        out_specs=(vmem,) * 3 + (hbm,) * 4,
        scratch_shapes=[
            pltpu.VMEM((2, 2 * n, 2 * n), F32),
            pltpu.VMEM((3, 2 * n, 2 * n), F32),
            pltpu.VMEM((frames, 2, n, n), F32),
            pltpu.VMEM((frames, 2, n, n), F32),
            pltpu.VMEM((2 * n, 2 * n), BF16),
            pltpu.VMEM((2 * n, 2 * n), BF16),
            pltpu.VMEM((2 * n, frames * n), BF16),
            pltpu.VMEM((frames * n, 2 * n), BF16),
            pltpu.VMEM((frames * n, 2 * n), F32),
            pltpu.SemaphoreType.DMA((4,)),
            pltpu.SemaphoreType.DMA((4,)),
        ],
        name="frames",
    )(core, positions, count, coefficients, *blocks, amplitudes, modes, *tables)


def spread_kernel(got_ref, out_ref):
    total = jnp.sum(got_ref[...], axis=0)
    out_ref[...] = jnp.broadcast_to(total[None], out_ref.shape)


def run_spread(got):
    vmem = pl.BlockSpec(memory_space=pltpu.VMEM)
    return pl.pallas_call(
        spread_kernel,
        out_shape=jax.ShapeDtypeStruct(got.shape, F32),
        in_specs=[vmem],
        out_specs=vmem,
        name="spread",
    )(got)


def total_of(acc):
    across = jnp.sum(jnp.sum(acc, axis=0, keepdims=True), axis=1, keepdims=True)
    return jnp.broadcast_to(across, acc.shape)


def modes_kernel(
    core_ref, cnt_ref, coef_ref, mine_ref, other_ref, old_ref, grads_ref, new_ref, out_coef_ref, raised_ref,
    *, root_total,
):
    modes, n = old_ref.shape[0], old_ref.shape[2]
    frames = grads_ref.shape[0]
    pixels = n * n
    is_first = core_ref[0] == 0
    lanes = n // 128
    pairs = [(i, j) for j in range(modes) for i in range(j)]
    zero = jnp.zeros((8, 128), F32)

    def lift(t, acc):
        acc = list(acc)
        at = pl.ds(pl.multiple_of(t * 8, 8), 8)
        for lane in range(lanes):
            col = slice(lane * 128, lane * 128 + 128)
            tile = t * lanes + lane
            re, im = [], []
            for k in range(modes):
                mine = mine_ref[tile, k]
                other = other_ref[tile, k]
                s_re = jnp.where(is_first, mine, other)
                s_im = jnp.where(is_first, other, mine)
                re.append(old_ref[k, 0, at, col] + s_re * (1.0 / root_total))
                im.append(old_ref[k, 1, at, col] + s_im * (1.0 / root_total))
                raised_ref[k, 0, at, col] = re[k]
                raised_ref[k, 1, at, col] = im[k]
            for k in range(modes):
                acc[k] = acc[k] + (re[k] * re[k] + im[k] * im[k])
            for p, (i, j) in enumerate(pairs):
                acc[modes + 2 * p] = acc[modes + 2 * p] + (re[i] * re[j] + im[i] * im[j])
                acc[modes + 2 * p + 1] = acc[modes + 2 * p + 1] + (re[i] * im[j] - im[i] * re[j])
        return tuple(acc)

    acc = lax.fori_loop(0, n // 8, lift, (zero,) * (modes + 2 * len(pairs)))
    gram = [total_of(a) * (1.0 / pixels) for a in acc]
    upper = {}
    inverse = []
    for j in range(modes):
        for i in range(j):
            p = pairs.index((i, j))
            s_re = gram[modes + 2 * p]
            s_im = gram[modes + 2 * p + 1]
            for k in range(i):
                a_re, a_im = upper[k, i]
                b_re, b_im = upper[k, j]
                s_re = s_re - (a_re * b_re + a_im * b_im)
                s_im = s_im - (a_re * b_im - a_im * b_re)
            upper[i, j] = (s_re * inverse[i], s_im * inverse[i])
        diagonal = gram[j]
        for k in range(j):
            a_re, a_im = upper[k, j]
            diagonal = diagonal - (a_re * a_re + a_im * a_im)
        inverse.append(1.0 / jnp.sqrt(diagonal))

    def solve(t, acc):
        acc = list(acc)
        at = pl.ds(pl.multiple_of(t * 8, 8), 8)
        for lane in range(lanes):
            col = slice(lane * 128, lane * 128 + 128)
            basis = []
            for j in range(modes):
                v_re = raised_ref[j, 0, at, col]
                v_im = raised_ref[j, 1, at, col]
                for i in range(j):
                    r_re, r_im = upper[i, j]
                    q_re, q_im = basis[i]
                    v_re = v_re - (r_re * q_re - r_im * q_im)
                    v_im = v_im - (r_re * q_im + r_im * q_re)
                basis.append((v_re * inverse[j], v_im * inverse[j]))
                new_ref[j, 0, at, col] = basis[j][0]
                new_ref[j, 1, at, col] = basis[j][1]
            for j in range(modes):
                o_re = old_ref[j, 0, at, col]
                o_im = old_ref[j, 1, at, col]
                for k in range(modes):
                    s = j * modes + k
                    acc[s] = acc[s] + (basis[k][0] * o_re + basis[k][1] * o_im)
            for f in range(frames):
                g_re = grads_ref[f, 0, at, col]
                g_im = grads_ref[f, 1, at, col]
                for k in range(modes):
                    s = (modes + f) * modes + k
                    acc[s] = acc[s] + (basis[k][0] * g_re + basis[k][1] * g_im)
        return tuple(acc)

    acc = lax.fori_loop(0, n // 8, solve, (zero,) * ((modes + frames) * modes))
    dots = [jnp.sum(a) * (1.0 / pixels) for a in acc]
    for f in range(frames):
        for k in range(modes):
            value = 0.5 * dots[(modes + f) * modes + k]
            for j in range(modes):
                value = value + coef_ref[f, j] * dots[j * modes + k]
            out_coef_ref[f, k] = jnp.where(f < cnt_ref[0], value, coef_ref[f, k])


def run_modes(core, count, coefficients, mine, other, old, grads, root_total):
    smem = pl.BlockSpec(memory_space=pltpu.SMEM)
    vmem = pl.BlockSpec(memory_space=pltpu.VMEM)
    return pl.pallas_call(
        functools.partial(modes_kernel, root_total=root_total),
        out_shape=(
            jax.ShapeDtypeStruct(old.shape, F32),
            jax.ShapeDtypeStruct(coefficients.shape, F32),
        ),
        in_specs=[smem] * 3 + [vmem] * 4,
        out_specs=(vmem, smem),
        scratch_shapes=[pltpu.VMEM(old.shape, F32)],
        name="modes",
    )(core, count, coefficients, mine, other, old, grads)


def moves(scans, cols, down, over):
    pairs = []
    for s in range(scans):
        for c in range(cols):
            if 0 <= s + down < scans and 0 <= c + over < cols:
                pairs.append((s * cols + c, (s + down) * cols + c + over))
    return pairs


def on_device(object_field, amplitudes, positions, frame_count, coefficients, probe_modes):
    frames, length = amplitudes.shape[0], amplitudes.shape[1]
    cols = lax.axis_size("y")
    scans = lax.axis_size(SCAN)
    root_total = math.sqrt(frames * scans * cols)
    core = lax.axis_index("core").astype(jnp.int32).reshape(1)
    swap = [(0, 1), (1, 0)]

    def widen(block):
        corner = lax.ppermute(block, ALL, moves(scans, cols, -1, -1))
        right = lax.ppermute(block, ALL, moves(scans, cols, 0, -1))
        below = lax.ppermute(block, ALL, moves(scans, cols, -1, 0))
        return [block, right, below, corner]

    tables = make_tables(length)
    blocks = widen(object_field)
    for iteration in range(ITERS):
        keep, give, grads, t_own, t_right, t_below, t_corner = run_frames(
            core, positions, frame_count, coefficients, blocks, amplitudes, probe_modes, tables
        )
        kept = keep + lax.ppermute(give, "core", swap)
        crossed = lax.ppermute(t_corner, ALL, moves(scans, cols, 1, 1))
        arrived = lax.ppermute(t_right, ALL, moves(scans, cols, 0, 1))
        lowered = lax.ppermute(t_below, ALL, moves(scans, cols, 1, 0))
        got = lax.all_to_all(kept, CHIPS, split_axis=0, concat_axis=0, tiled=True)
        settled = t_own + arrived + lowered + crossed
        object_field = object_field + settled[:2] / (settled[2] + 1.0)
        if iteration + 1 < ITERS:
            blocks = widen(object_field)
            got, object_field = lax.optimization_barrier((got, object_field))
        spread = run_spread(got)
        mine = lax.all_to_all(spread, CHIPS, split_axis=0, concat_axis=0, tiled=True)
        other = lax.ppermute(mine, "core", swap)
        probe_modes, coefficients = run_modes(
            core, frame_count, coefficients, mine, other, probe_modes, grads, root_total
        )
    return (object_field, probe_modes, coefficients)


def solution(mesh):
    scans, cols = mesh.shape["scan"], mesh.shape["col"]
    fine = Mesh(np.asarray(mesh.devices).reshape(4, scans // 8, 2, cols), ALL)
    placed = (
        P(None, SCAN, "y"),
        P(ALL, None, None),
        P(ALL, None),
        P(ALL),
        P(ALL, None),
        P(),
    )
    return jax.shard_map(
        on_device,
        mesh=fine,
        in_specs=placed,
        out_specs=(P(None, SCAN, "y"), P(), P(ALL, None)),
        check_vma=False,
    )
```

profile of v0, /device:TPU:25, one launch (start us, length us, event | category | flops | bytes accessed | tf_op | source)
XLA Modules:
  0.0 254.0 jit_solution(5070380360380766224)
XLA Ops:
  0.6 3.0 %collective-permute-start.2 = (f32[2,256,256]{2,1,0:T(8,128)}, f32[2,256,256]{2,1,0:T(8,128)S(1)}, u32[]{:S(2)}, u32[]{:S(2)}) collective-permute-start(f32[2,256,256]{2,1,0:T(8,128)} %own_ref.1), channel_id=1, source_target_pairs={{5,0},{6,1},{7,2},{9,4},{10,5},{11,6},{13,8},{14,9},{15,10},{17,12... | collective-permute-start | bytes 1572872 | tf_op jit(solution)/shard_map/ppermute | solution.py:371
  3.6 1.9 collective-permute-start.1
  5.5 2.1 collective-permute-start
  8.3 1.8 multiply_convert_fusion
  10.0 10.2 %collective-permute-done.2.corner_ref = f32[2,256,256]{2,1,0:T(8,128)S(1)} collective-permute-done((f32[2,256,256]{2,1,0:T(8,128)}, f32[2,256,256]{2,1,0:T(8,128)S(1)}, u32[]{:S(2)}, u32[]{:S(2)}) %collective-permute-start.2) | collective-permute-done | bytes 524320 | tf_op jit(solution)/shard_map/ppermute | solution.py:371
  20.2 0.0 collective-permute-done.1.below_ref
  20.2 6.6 %collective-permute-done.right_ref = f32[2,256,256]{2,1,0:T(8,128)S(1)} collective-permute-done((f32[2,256,256]{2,1,0:T(8,128)}, f32[2,256,256]{2,1,0:T(8,128)S(1)}, u32[]{:S(2)}, u32[]{:S(2)}) %collective-permute-start) | collective-permute-done | bytes 524320 | tf_op jit(solution)/shard_map/ppermute | solution.py:372
  26.8 0.0 copy-done.10
  26.8 0.0 copy-done.12
  26.9 0.8 copy-done.13
  27.6 11.3 %frames.2 = (f32[64,4,8,128]{3,2,1,0:T(8,128)}, f32[64,4,8,128]{3,2,1,0:T(8,128)}, f32[2,2,256,256]{3,2,1,0:T(8,128)}, f32[3,256,256]{2,1,0:T(8,128)}, f32[3,256...) custom-call(s32[1]{0:T(128)} %bitcast.core_ref, s32[2,2]{1,0:T(2,128)} %pos_ref.3, ...), custom_call_target="tpu_custom_call" | custom-call | tf_op jit(solution)/shard_map/frames/pallas_call | solution.py:197
  39.0 0.1 collective-permute-start.3
  39.1 1.3 collective-permute-start.4
  40.4 3.5 %collective-permute-start.5 = (f32[3,256,256]{2,1,0:T(8,128)}, f32[3,256,256]{2,1,0:T(8,128)}, u32[]{:S(2)}, u32[]{:S(2)}) collective-permute-start(f32[3,256,256]{2,1,0:T(8,128)} %get-tuple-element.27), channel_id=1, source_target_pairs={{0,4},{1,5},{2,6},{3,7},{4,8},{5,9},{6,10},{7,11},{8,12},{9,13},{1... | collective-permute-start | bytes 2359304 | tf_op jit(solution)/shard_map/ppermute | solution.py:385
  43.9 1.3 collective-permute-start.6
  45.2 0.0 collective-permute-done.3
  45.2 0.0 copy-start.9
  45.2 2.5 add.51
  47.7 13.7 %all-to-all-start = ((f32[64,4,8,128]{3,2,1,0:T(8,128)}), f32[64,4,8,128]{3,2,1,0:T(8,128)S(1)}, u32[]{:S(2)}, u32[]{:S(2)}) async-start(f32[64,4,8,128]{3,2,1,0:T(8,128)} %add.51), calls=%async_computation | async-start | bytes 2097152 | tf_op jit(solution)/shard_map/all_to_all | solution.py:386
  61.4 14.6 %collective-permute-done.4 = f32[3,256,256]{2,1,0:T(8,128)S(1)} collective-permute-done((f32[3,256,256]{2,1,0:T(8,128)}, f32[3,256,256]{2,1,0:T(8,128)S(1)}, u32[]{:S(2)}, u32[]{:S(2)}) %collective-permute-start.4) | collective-permute-done | bytes 786464 | tf_op jit(solution)/shard_map/ppermute | solution.py:384
  76.0 0.0 collective-permute-done.5
  76.0 11.6 %collective-permute-done.6 = f32[3,256,256]{2,1,0:T(8,128)} collective-permute-done((f32[3,256,256]{2,1,0:T(8,128)}, f32[3,256,256]{2,1,0:T(8,128)}, u32[]{:S(2)}, u32[]{:S(2)}) %collective-permute-start.6) | collective-permute-done | bytes 786464 | tf_op jit(solution)/shard_map/ppermute | solution.py:383
  87.6 0.0 copy-done.9
  87.6 1.6 add_add_fusion.1
  89.2 0.0 copy-done.5
  89.3 0.1 fusion.1.own_ref
  89.3 0.0 copy-start
  89.4 0.0 all-to-all-done.got_ref
  89.4 0.0 copy-start.4
  89.4 1.0 copy-done.4
  90.4 2.4 spread.2
  92.8 28.0 %all_to_all.20.mine_ref = f32[64,4,8,128]{3,2,1,0:T(8,128)S(1)} all-to-all(f32[64,4,8,128]{3,2,1,0:T(8,128)} %spread.2), channel_id=1, replica_groups=mesh['z'=4,'x'=4,'core'=2,'y'=4] {'z','x','y'}, dimensions={0} | all-to-all | bytes 2097152 | tf_op jit(solution)/shard_map/all_to_all | solution.py:393
  120.8 1.7 collective-permute-start.7
  122.5 2.5 collective-permute-start.10
  124.9 1.9 collective-permute-start.9
  126.9 4.2 %collective-permute-start.8 = (f32[2,256,256]{2,1,0:T(8,128)S(1)}, f32[2,256,256]{2,1,0:T(8,128)}, u32[]{:S(2)}, u32[]{:S(2)}) collective-permute-start(f32[2,256,256]{2,1,0:T(8,128)S(1)} %fusion.1.own_ref), channel_id=1, source_target_pairs={{1,0},{2,1},{3,2},{5,4},{6,5},{7,6},{9,8},{10,9},{11,10},{13,12},{... | collective-permute-start | bytes 1572872 | tf_op jit(solution)/shard_map/ppermute | solution.py:372
  131.0 0.0 collective-permute-done.7.other_ref
  131.0 0.0 copy-done.3
  131.0 1.0 copy-done.7
  132.0 6.7 %modes.2 = (f32[4,2,256,256]{3,2,1,0:T(8,128)}, f32[2,4]{1,0:T(2,128)}) custom-call(s32[1]{0:T(128)} %bitcast.core_ref, s32[1]{0:T(128)S(6)} %copy.9.cnt_ref, f32[2,4]{1,0:T(2,128)} %coef_ref.3, f32[64,4,8,128]{3,2,1,0:T(8,128)} %copy-done.3, f32[64,4,8,128]{3,2,1,0:T(8,128)} %copy-done.7, f32[4,2,256,256]{3,2,1,0:T(8,128)} %old_ref.1, ...), custom_call_target="tpu_custom_call" | custom-call | tf_op jit(solution)/shard_map/modes/pallas_call | solution.py:340
  138.8 1.8 collective-permute-done.10.corner_ref
  140.6 0.0 collective-permute-done.9.below_ref
  140.6 7.3 %collective-permute-done.8.right_ref = f32[2,256,256]{2,1,0:T(8,128)} collective-permute-done((f32[2,256,256]{2,1,0:T(8,128)S(1)}, f32[2,256,256]{2,1,0:T(8,128)}, u32[]{:S(2)}, u32[]{:S(2)}) %collective-permute-start.8) | collective-permute-done | bytes 524320 | tf_op jit(solution)/shard_map/ppermute | solution.py:372
  147.9 0.0 copy-done.11
  147.9 11.3 %frames.3 = (f32[64,4,8,128]{3,2,1,0:T(8,128)}, f32[64,4,8,128]{3,2,1,0:T(8,128)}, f32[2,2,256,256]{3,2,1,0:T(8,128)}, f32[3,256,256]{2,1,0:T(8,128)}, f32[3,256...) custom-call(s32[1]{0:T(128)} %bitcast.core_ref, s32[2,2]{1,0:T(2,128)} %pos_ref.3, ...), custom_call_target="tpu_custom_call" | custom-call | tf_op jit(solution)/shard_map/frames/pallas_call | solution.py:197
  159.2 0.1 collective-permute-start.14
  159.3 2.9 %collective-permute-done.14 = f32[64,4,8,128]{3,2,1,0:T(8,128)S(1)} collective-permute-done((f32[64,4,8,128]{3,2,1,0:T(8,128)}, f32[64,4,8,128]{3,2,1,0:T(8,128)S(1)}, u32[]{:S(2)}, u32[]{:S(2)}) %collective-permute-start.14) | collective-permute-done | bytes 1048608 | tf_op jit(solution)/shard_map/ppermute | solution.py:382
  162.1 1.4 add.62
  163.6 23.9 %all_to_all.21.got_ref = f32[64,4,8,128]{3,2,1,0:T(8,128)} all-to-all(f32[64,4,8,128]{3,2,1,0:T(8,128)S(1)} %add.62), channel_id=1, replica_groups=mesh['z'=4,'x'=4,'core'=2,'y'=4] {'z','x','y'}, dimensions={0} | all-to-all | bytes 2097152 | tf_op jit(solution)/shard_map/all_to_all | solution.py:386
  187.4 2.5 spread.3
  189.9 6.6 %all-to-all-start.3 = ((f32[64,4,8,128]{3,2,1,0:T(8,128)}), f32[64,4,8,128]{3,2,1,0:T(8,128)S(1)}, u32[]{:S(2)}, u32[]{:S(2)}) async-start(f32[64,4,8,128]{3,2,1,0:T(8,128)} %spread.3), calls=%async_computation.3 | async-start | bytes 2097152 | tf_op jit(solution)/shard_map/all_to_all | solution.py:393
  196.5 1.3 collective-permute-start.11
  197.8 5.0 %collective-permute-start.12 = (f32[3,256,256]{2,1,0:T(8,128)}, f32[3,256,256]{2,1,0:T(8,128)}, u32[]{:S(2)}, u32[]{:S(2)}) collective-permute-start(f32[3,256,256]{2,1,0:T(8,128)} %get-tuple-element.36), channel_id=1, source_target_pairs={{0,4},{1,5},{2,6},{3,7},{4,8},{5,9},{6,10},{7,11},{8,12},{9,13},{1... | collective-permute-start | bytes 2359304 | tf_op jit(solution)/shard_map/ppermute | solution.py:385
  202.9 1.3 collective-permute-start.13
  204.2 7.2 %all-to-all-done.3.mine_ref = f32[64,4,8,128]{3,2,1,0:T(8,128)S(1)} async-done(((f32[64,4,8,128]{3,2,1,0:T(8,128)}), f32[64,4,8,128]{3,2,1,0:T(8,128)S(1)}, u32[]{:S(2)}, u32[]{:S(2)}) %all-to-all-start.3) | async-done | bytes 1048608 | tf_op jit(solution)/shard_map/all_to_all | solution.py:393
  211.4 3.1 %collective-permute-start.15 = (f32[64,4,8,128]{3,2,1,0:T(8,128)S(1)}, f32[64,4,8,128]{3,2,1,0:T(8,128)S(1)}, u32[]{:S(2)}, u32[]{:S(2)}) collective-permute-start(f32[64,4,8,128]{3,2,1,0:T(8,128)S(1)} %all-to-all-done.3.mine_ref), channel_id=1, source_target_pairs={{0,4},{4,0},{1,5},{5,1},{2,6},{6,2},{3,7},{7,3},{8,12},{12,8},{9,1... | collective-permute-start | bytes 3145736 | tf_op jit(solution)/shard_map/ppermute | solution.py:394
  214.5 19.6 %collective-permute-done.11 = f32[3,256,256]{2,1,0:T(8,128)} collective-permute-done((f32[3,256,256]{2,1,0:T(8,128)}, f32[3,256,256]{2,1,0:T(8,128)}, u32[]{:S(2)}, u32[]{:S(2)}) %collective-permute-start.11) | collective-permute-done | bytes 786464 | tf_op jit(solution)/shard_map/ppermute | solution.py:384
  234.1 0.0 collective-permute-done.12
  234.1 9.3 %collective-permute-done.13 = f32[3,256,256]{2,1,0:T(8,128)} collective-permute-done((f32[3,256,256]{2,1,0:T(8,128)}, f32[3,256,256]{2,1,0:T(8,128)}, u32[]{:S(2)}, u32[]{:S(2)}) %collective-permute-start.13) | collective-permute-done | bytes 786464 | tf_op jit(solution)/shard_map/ppermute | solution.py:383
  243.4 1.9 add_add_fusion
  245.4 0.9 fusion
  246.2 0.0 collective-permute-done.15.other_ref
  246.2 1.0 copy-done.6
  247.3 6.7 %modes.3 = (f32[4,2,256,256]{3,2,1,0:T(8,128)}, f32[2,4]{1,0:T(2,128)}) custom-call(s32[1]{0:T(128)} %bitcast.core_ref, s32[1]{0:T(128)S(6)} %copy.9.cnt_ref, f32[2,4]{1,0:T(2,128)} %get-tuple-element.32.coef_ref, f32[64,4,8,128]{3,2,1,0:T(8,128)} %copy-done.2, f32[64,4,8,128]{3,2,1,0:T(8,128)} %copy-done.6, ...), custom_call_target="tpu_custom_call" | custom-call | tf_op jit(solution)/shard_map/modes/pallas_call | solution.py:340
  (17 shorter events, 0.1 us)
Async XLA Ops:
  0.6 19.6 %collective-permute-start.2 = (f32[2,256,256]{2,1,0:T(8,128)}, f32[2,256,256]{2,1,0:T(8,128)S(1)}, u32[]{:S(2)}, u32[]{:S(2)}) collective-permute-start(f32[2,256,256]{2,1,0:T(8,128)} %own_ref.1), channel_id=1, source_target_pairs={{5,0},{6,1},{7,2},{9,4},{10,5},{11,6},{13,8},{14,9},{15,10},{17,12... | collective-permute-start | bytes 1572872 | tf_op jit(solution)/shard_map/ppermute | solution.py:371
  3.6 16.6 %collective-permute-start.1 = (f32[2,256,256]{2,1,0:T(8,128)}, f32[2,256,256]{2,1,0:T(8,128)S(1)}, u32[]{:S(2)}, u32[]{:S(2)}) collective-permute-start(f32[2,256,256]{2,1,0:T(8,128)} %own_ref.1), channel_id=1, source_target_pairs={{4,0},{5,1},{6,2},{7,3},{8,4},{9,5},{10,6},{11,7},{12,8},{13,9},{1... | collective-permute-start | bytes 1572872 | tf_op jit(solution)/shard_map/ppermute | solution.py:373
  5.5 21.3 %collective-permute-start = (f32[2,256,256]{2,1,0:T(8,128)}, f32[2,256,256]{2,1,0:T(8,128)S(1)}, u32[]{:S(2)}, u32[]{:S(2)}) collective-permute-start(f32[2,256,256]{2,1,0:T(8,128)} %own_ref.1), channel_id=1, source_target_pairs={{1,0},{2,1},{3,2},{5,4},{6,5},{7,6},{9,8},{10,9},{11,10},{13,12},{... | collective-permute-start | bytes 1572872 | tf_op jit(solution)/shard_map/ppermute | solution.py:372
  20.2 6.6 %copy-start.10 = (f32[2,256,256]{2,1,0:T(8,128)}, f32[2,256,256]{2,1,0:T(8,128)S(1)}, u32[]{:S(2)}) copy-start(f32[2,256,256]{2,1,0:T(8,128)S(1)} %collective-permute-done.2.corner_ref) | copy-start | bytes 1572868
  20.2 6.6 %copy-start.12 = (f32[2,256,256]{2,1,0:T(8,128)}, f32[2,256,256]{2,1,0:T(8,128)S(1)}, u32[]{:S(2)}) copy-start(f32[2,256,256]{2,1,0:T(8,128)S(1)} %collective-permute-done.1.below_ref) | copy-start | bytes 1572868
  26.8 0.8 copy-start.13
  39.0 6.2 %collective-permute-start.3 = (f32[64,4,8,128]{3,2,1,0:T(8,128)}, f32[64,4,8,128]{3,2,1,0:T(8,128)S(1)}, u32[]{:S(2)}, u32[]{:S(2)}) collective-permute-start(f32[64,4,8,128]{3,2,1,0:T(8,128)} %get-tuple-element.24), channel_id=1, source_target_pairs={{0,4},{4,0},{1,5},{5,1},{2,6},{6,2},{3,7},{7,3},{8,12},{12,8},{9,1... | collective-permute-start | bytes 3145736 | tf_op jit(solution)/shard_map/ppermute | solution.py:382
  39.1 37.0 %collective-permute-start.4 = (f32[3,256,256]{2,1,0:T(8,128)}, f32[3,256,256]{2,1,0:T(8,128)S(1)}, u32[]{:S(2)}, u32[]{:S(2)}) collective-permute-start(f32[3,256,256]{2,1,0:T(8,128)} %get-tuple-element.26), channel_id=1, source_target_pairs={{0,1},{1,2},{2,3},{4,5},{5,6},{6,7},{8,9},{9,10},{10,11},{12,13},{... | collective-permute-start | bytes 2359304 | tf_op jit(solution)/shard_map/ppermute | solution.py:384
  40.4 35.7 %collective-permute-start.5 = (f32[3,256,256]{2,1,0:T(8,128)}, f32[3,256,256]{2,1,0:T(8,128)}, u32[]{:S(2)}, u32[]{:S(2)}) collective-permute-start(f32[3,256,256]{2,1,0:T(8,128)} %get-tuple-element.27), channel_id=1, source_target_pairs={{0,4},{1,5},{2,6},{3,7},{4,8},{5,9},{6,10},{7,11},{8,12},{9,13},{1... | collective-permute-start | bytes 2359304 | tf_op jit(solution)/shard_map/ppermute | solution.py:385
  43.9 43.7 %collective-permute-start.6 = (f32[3,256,256]{2,1,0:T(8,128)}, f32[3,256,256]{2,1,0:T(8,128)}, u32[]{:S(2)}, u32[]{:S(2)}) collective-permute-start(f32[3,256,256]{2,1,0:T(8,128)} %get-tuple-element.28), channel_id=1, source_target_pairs={{0,5},{1,6},{2,7},{4,9},{5,10},{6,11},{8,13},{9,14},{10,15},{12,17... | collective-permute-start | bytes 2359304 | tf_op jit(solution)/shard_map/ppermute | solution.py:383
  45.2 42.4 %copy-start.9 = (f32[3,256,256]{2,1,0:T(8,128)S(1)}, f32[3,256,256]{2,1,0:T(8,128)}, u32[]{:S(2)}) copy-start(f32[3,256,256]{2,1,0:T(8,128)} %get-tuple-element.25) | copy-start | bytes 2359300
  47.7 41.7 %all-to-all-start = ((f32[64,4,8,128]{3,2,1,0:T(8,128)}), f32[64,4,8,128]{3,2,1,0:T(8,128)S(1)}, u32[]{:S(2)}, u32[]{:S(2)}) async-start(f32[64,4,8,128]{3,2,1,0:T(8,128)} %add.51), calls=%async_computation | async-start | bytes 2097152 | tf_op jit(solution)/shard_map/all_to_all | solution.py:386
  87.6 1.7 copy-start.5
  89.3 37.5 %copy-start = (f32[2,256,256]{2,1,0:T(8,128)}, f32[2,256,256]{2,1,0:T(8,128)S(1)}, u32[]{:S(2)}) copy-start(f32[2,256,256]{2,1,0:T(8,128)S(1)} %fusion.1.own_ref) | copy-start | bytes 1572868
  89.4 1.0 copy-start.4
  120.8 10.3 %copy-start.3 = (f32[64,4,8,128]{3,2,1,0:T(8,128)}, f32[64,4,8,128]{3,2,1,0:T(8,128)S(1)}, u32[]{:S(2)}) copy-start(f32[64,4,8,128]{3,2,1,0:T(8,128)S(1)} %all_to_all.20.mine_ref) | copy-start | bytes 3145732
  120.8 10.3 %collective-permute-start.7 = (f32[64,4,8,128]{3,2,1,0:T(8,128)S(1)}, f32[64,4,8,128]{3,2,1,0:T(8,128)S(1)}, u32[]{:S(2)}, u32[]{:S(2)}) collective-permute-start(f32[64,4,8,128]{3,2,1,0:T(8,128)S(1)} %all_to_all.20.mine_ref), channel_id=1, source_target_pairs={{0,4},{4,0},{1,5},{5,1},{2,6},{6,2},{3,7},{7,3},{8,12},{12,8},{9,1... | collective-permute-start | bytes 3145736 | tf_op jit(solution)/shard_map/ppermute | solution.py:394
  122.5 18.1 %collective-permute-start.10 = (f32[2,256,256]{2,1,0:T(8,128)S(1)}, f32[2,256,256]{2,1,0:T(8,128)S(1)}, u32[]{:S(2)}, u32[]{:S(2)}) collective-permute-start(f32[2,256,256]{2,1,0:T(8,128)S(1)} %fusion.1.own_ref), channel_id=1, source_target_pairs={{5,0},{6,1},{7,2},{9,4},{10,5},{11,6},{13,8},{14,9},{15,10},{17,12... | collective-permute-start | bytes 1572872 | tf_op jit(solution)/shard_map/ppermute | solution.py:371
  124.9 15.6 %collective-permute-start.9 = (f32[2,256,256]{2,1,0:T(8,128)S(1)}, f32[2,256,256]{2,1,0:T(8,128)}, u32[]{:S(2)}, u32[]{:S(2)}) collective-permute-start(f32[2,256,256]{2,1,0:T(8,128)S(1)} %fusion.1.own_ref), channel_id=1, source_target_pairs={{4,0},{5,1},{6,2},{7,3},{8,4},{9,5},{10,6},{11,7},{12,8},{13,9},{1... | collective-permute-start | bytes 1572872 | tf_op jit(solution)/shard_map/ppermute | solution.py:373
  126.9 21.0 %collective-permute-start.8 = (f32[2,256,256]{2,1,0:T(8,128)S(1)}, f32[2,256,256]{2,1,0:T(8,128)}, u32[]{:S(2)}, u32[]{:S(2)}) collective-permute-start(f32[2,256,256]{2,1,0:T(8,128)S(1)} %fusion.1.own_ref), channel_id=1, source_target_pairs={{1,0},{2,1},{3,2},{5,4},{6,5},{7,6},{9,8},{10,9},{11,10},{13,12},{... | collective-permute-start | bytes 1572872 | tf_op jit(solution)/shard_map/ppermute | solution.py:372
  131.0 1.0 copy-start.7
  140.6 7.3 %copy-start.11 = (f32[2,256,256]{2,1,0:T(8,128)}, f32[2,256,256]{2,1,0:T(8,128)S(1)}, u32[]{:S(2)}) copy-start(f32[2,256,256]{2,1,0:T(8,128)S(1)} %collective-permute-done.10.corner_ref) | copy-start | bytes 1572868
  159.2 3.0 %collective-permute-start.14 = (f32[64,4,8,128]{3,2,1,0:T(8,128)}, f32[64,4,8,128]{3,2,1,0:T(8,128)S(1)}, u32[]{:S(2)}, u32[]{:S(2)}) collective-permute-start(f32[64,4,8,128]{3,2,1,0:T(8,128)} %get-tuple-element.39), channel_id=1, source_target_pairs={{0,4},{4,0},{1,5},{5,1},{2,6},{6,2},{3,7},{7,3},{8,12},{12,8},{9,1... | collective-permute-start | bytes 3145736 | tf_op jit(solution)/shard_map/ppermute | solution.py:382
  187.4 56.0 %copy-start.8 = (f32[3,256,256]{2,1,0:T(8,128)S(1)}, f32[3,256,256]{2,1,0:T(8,128)}, u32[]{:S(2)}) copy-start(f32[3,256,256]{2,1,0:T(8,128)} %get-tuple-element.34) | copy-start | bytes 2359300
  189.9 21.5 %all-to-all-start.3 = ((f32[64,4,8,128]{3,2,1,0:T(8,128)}), f32[64,4,8,128]{3,2,1,0:T(8,128)S(1)}, u32[]{:S(2)}, u32[]{:S(2)}) async-start(f32[64,4,8,128]{3,2,1,0:T(8,128)} %spread.3), calls=%async_computation.3 | async-start | bytes 2097152 | tf_op jit(solution)/shard_map/all_to_all | solution.py:393
  196.5 37.6 %collective-permute-start.11 = (f32[3,256,256]{2,1,0:T(8,128)}, f32[3,256,256]{2,1,0:T(8,128)}, u32[]{:S(2)}, u32[]{:S(2)}) collective-permute-start(f32[3,256,256]{2,1,0:T(8,128)} %get-tuple-element.35), channel_id=1, source_target_pairs={{0,1},{1,2},{2,3},{4,5},{5,6},{6,7},{8,9},{9,10},{10,11},{12,13},{... | collective-permute-start | bytes 2359304 | tf_op jit(solution)/shard_map/ppermute | solution.py:384
  197.8 36.3 %collective-permute-start.12 = (f32[3,256,256]{2,1,0:T(8,128)}, f32[3,256,256]{2,1,0:T(8,128)}, u32[]{:S(2)}, u32[]{:S(2)}) collective-permute-start(f32[3,256,256]{2,1,0:T(8,128)} %get-tuple-element.36), channel_id=1, source_target_pairs={{0,4},{1,5},{2,6},{3,7},{4,8},{5,9},{6,10},{7,11},{8,12},{9,13},{1... | collective-permute-start | bytes 2359304 | tf_op jit(solution)/shard_map/ppermute | solution.py:385
  202.9 40.6 %collective-permute-start.13 = (f32[3,256,256]{2,1,0:T(8,128)}, f32[3,256,256]{2,1,0:T(8,128)}, u32[]{:S(2)}, u32[]{:S(2)}) collective-permute-start(f32[3,256,256]{2,1,0:T(8,128)} %get-tuple-element.37), channel_id=1, source_target_pairs={{0,5},{1,6},{2,7},{4,9},{5,10},{6,11},{8,13},{9,14},{10,15},{12,17... | collective-permute-start | bytes 2359304 | tf_op jit(solution)/shard_map/ppermute | solution.py:383
  211.4 33.9 %copy-start.2 = (f32[64,4,8,128]{3,2,1,0:T(8,128)}, f32[64,4,8,128]{3,2,1,0:T(8,128)S(1)}, u32[]{:S(2)}) copy-start(f32[64,4,8,128]{3,2,1,0:T(8,128)S(1)} %all-to-all-done.3.mine_ref) | copy-start | bytes 3145732
  211.4 34.8 %collective-permute-start.15 = (f32[64,4,8,128]{3,2,1,0:T(8,128)S(1)}, f32[64,4,8,128]{3,2,1,0:T(8,128)S(1)}, u32[]{:S(2)}, u32[]{:S(2)}) collective-permute-start(f32[64,4,8,128]{3,2,1,0:T(8,128)S(1)} %all-to-all-done.3.mine_ref), channel_id=1, source_target_pairs={{0,4},{4,0},{1,5},{5,1},{2,6},{6,2},{3,7},{7,3},{8,12},{12,8},{9,1... | collective-permute-start | bytes 3145736 | tf_op jit(solution)/shard_map/ppermute | solution.py:394
  243.4 1.9 copy-start.1
  246.2 1.0 copy-start.6
where the time goes:
time: 255 us; the launch traced here: 254 us
  waiting for transfers between devices  91.1 us (36%)
  starting transfers between devices  54.5 us (21%)
  blocking collectives  51.9 us (20%)
  Pallas kernels  40.9 us (16%)
  other arithmetic  10.2 us (4%)
  local copies, waits for them, and re-layouts  3.83 us (2%)
    ppermute x2, waiting for transfers between devices, on_device(): arrived = lax.ppermute(t_right, ALL, moves(scans, cols, 0, 1))  34.2 us
    all_to_all x1, blocking collectives, on_device(): lax.all_to_all(spread, CHIPS, split_axis=0, concat_axis=0, tiled=True)  28 us
    all_to_all x1, blocking collectives, on_device(): got = lax.all_to_all(kept, CHIPS, split_axis=0, concat_axis=0, tiled=True)  23.9 us
    pallas_call x2, Pallas kernels, run_frames(): pl.pallas_call(frames_kernel, out_shape=(piece, piece, jax.ShapeDtypeStru...  22.7 us
    ppermute x2, waiting for transfers between devices, on_device(): crossed = lax.ppermute(t_corner, ALL, moves(scans, cols, 1, 1))  20.9 us
    ppermute x2, waiting for transfers between devices, widen(): right = lax.ppermute(block, ALL, moves(scans, cols, 0, -1))  13.9 us
    all_to_all x1, starting transfers between devices, on_device(): got = lax.all_to_all(kept, CHIPS, split_axis=0, concat_axis=0, tiled=True)  13.7 us
    pallas_call x2, Pallas kernels, run_modes(): pl.pallas_call(functools.partial(modes_kernel, root_total=root_total), ou...  13.4 us
  transfers between devices with their start and end apart: 18, of which 10 were waited for; matrix products, arithmetic and copies ran while one was open for 3% of the time, Pallas kernels for 3%

commit v1 on v0

--- a/solution.py
+++ b/solution.py
@@ -44,7 +44,7 @@
 
 
 def frames_kernel(
-    core_ref, pos_ref, cnt_ref, coef_ref, own_ref, right_ref, below_ref, corner_ref,
+    core_ref, pos_ref, cnt_ref, coef_ref, own_ref, right_ref, below_ref, corner_ref, beyond_ref,
     amp_ref, modes_ref, cos_ref, sin_ref,
     keep_ref, give_ref, grads_ref, t_own_ref, t_right_ref, t_below_ref, t_corner_ref,
     ext_ref, tot_ref, probe_ref, exit_ref, rows_ref, cols_ref, stack_ref, side_ref, wide_ref,
@@ -52,51 +52,89 @@
 ):
     frames, n = amp_ref.shape[0], amp_ref.shape[1]
     modes = modes_ref.shape[0]
-    loads = []
-    for i, (src, a, b) in enumerate(
-        ((own_ref, 0, 0), (right_ref, 0, n), (below_ref, n, 0), (corner_ref, n, n))
-    ):
-        loads.append(pltpu.make_async_copy(src, ext_ref.at[:, a : a + n, b : b + n], in_sem.at[i]))
-    for load in loads:
-        load.start()
+    lanes = n // 128
+    is_first = core_ref[0] == 0
+
+    def quarter(ref, a, b, lane):
+        return ref.at[:, b + lane, pl.ds(a, n), :]
+
+    def strip(ref, lane):
+        return ref.at[:, :, pl.ds(lane * 128, 128)]
+
+    def load(i, src, a, b):
+        return [
+            pltpu.make_async_copy(strip(src, lane), quarter(ext_ref, a, b, lane), in_sem.at[i * lanes + lane])
+            for lane in range(lanes)
+        ]
+
+    loads = load(0, own_ref, 0, 0) + load(1, right_ref, 0, lanes) + load(2, below_ref, n, 0)
+    for copy in loads:
+        copy.start()
+
+    @pl.when(is_first)
+    def _():
+        for copy in load(3, beyond_ref, n, lanes):
+            copy.start()
+
+    @pl.when(jnp.logical_not(is_first))
+    def _():
+        for copy in load(3, corner_ref, n, lanes):
+            copy.start()
+
     fill_tables(cos_ref, sin_ref, rows_ref, cols_ref)
-    tot_ref[...] = jnp.zeros_like(tot_ref)
-    is_first = core_ref[0] == 0
-    offsets = [(pos_ref[f, 0] & (n - 1), pos_ref[f, 1] & (n - 1)) for f in range(frames)]
+
+    def clear(t, carry):
+        at = pl.ds(pl.multiple_of(t * 32, 32), 32)
+        for q in range(3):
+            for lane in range(2 * lanes):
+                tot_ref[q, lane, at, :] = jnp.zeros((32, 128), F32)
+        return carry
+
+    lax.fori_loop(0, 2 * n // 32, clear, 0)
+    offsets = []
+    for f in range(frames):
+        r, c = pos_ref[f, 0] & (n - 1), pos_ref[f, 1] & (n - 1)
+        offsets.append((r, c >> 7, c & 127))
     weights = [
         [jnp.where(f < cnt_ref[0], coef_ref[f, k], 0.0) for k in range(modes)] for f in range(frames)
     ]
-    for load in loads:
-        load.wait()
+    column = lax.broadcasted_iota(jnp.int32, (ROWS, 128), 1)
+    for copy in loads + load(3, corner_ref, n, lanes):
+        copy.wait()
 
     def patch_rows(f, plane, b):
-        r, c = offsets[f]
-        base = pl.multiple_of((r >> 3) * 8 + b * ROWS, 8)
-        rows = ext_ref[plane, pl.ds(base, ROWS + 8), :]
-        rows = pltpu.roll(rows, (2 * n - c) & (2 * n - 1), 1)[:, :n]
-        return pltpu.roll(rows, ROWS + 8 - (r & 7), 0)[:ROWS]
+        r, tile, shift = offsets[f]
+        at = pl.ds(r + b * ROWS, ROWS)
+        back = (128 - shift) & 127
+        turned = [pltpu.roll(ext_ref[plane, tile + t, at, :], back, 1) for t in range(lanes + 1)]
+        return [jnp.where(column < 128 - shift, turned[t], turned[t + 1]) for t in range(lanes)]
 
     def start(b, carry):
         at = pl.ds(pl.multiple_of(b * ROWS, ROWS), ROWS)
         at_imag = pl.ds(pl.multiple_of(n + b * ROWS, ROWS), ROWS)
         for f in range(frames):
-            o_re = patch_rows(f, 0, b)
-            o_im = patch_rows(f, 1, b)
-            grads_ref[f, 0, at, :] = o_re
-            grads_ref[f, 1, at, :] = o_im
-            p_re = weights[f][0] * modes_ref[0, 0, at, :]
-            p_im = weights[f][0] * modes_ref[0, 1, at, :]
-            for k in range(1, modes):
-                p_re = p_re + weights[f][k] * modes_ref[k, 0, at, :]
-                p_im = p_im + weights[f][k] * modes_ref[k, 1, at, :]
-            probe_ref[f, 0, at, :] = p_re
-            probe_ref[f, 1, at, :] = p_im
-            e_re = p_re * o_re - p_im * o_im
-            e_im = p_re * o_im + p_im * o_re
-            exit_ref[f, 0, at, :] = e_re
-            exit_ref[f, 1, at, :] = e_im
-            stack_ref[at, f * n : (f + 1) * n] = e_re.astype(BF16)
-            stack_ref[at_imag, f * n : (f + 1) * n] = e_im.astype(BF16)
+            reals = patch_rows(f, 0, b)
+            imags = patch_rows(f, 1, b)
+            for lane in range(lanes):
+                col = slice(lane * 128, lane * 128 + 128)
+                col_f = slice(f * n + lane * 128, f * n + lane * 128 + 128)
+                o_re = reals[lane]
+                o_im = imags[lane]
+                grads_ref[f, 0, at, col] = o_re
+                grads_ref[f, 1, at, col] = o_im
+                p_re = weights[f][0] * modes_ref[0, 0, at, col]
+                p_im = weights[f][0] * modes_ref[0, 1, at, col]
+                for k in range(1, modes):
+                    p_re = p_re + weights[f][k] * modes_ref[k, 0, at, col]
+                    p_im = p_im + weights[f][k] * modes_ref[k, 1, at, col]
+                probe_ref[f, 0, at, col] = p_re
+                probe_ref[f, 1, at, col] = p_im
+                e_re = p_re * o_re - p_im * o_im
+                e_im = p_re * o_im + p_im * o_re
+                exit_ref[f, 0, at, col] = e_re
+                exit_ref[f, 1, at, col] = e_im
+                stack_ref[at, col_f] = e_re.astype(BF16)
+                stack_ref[at_imag, col_f] = e_im.astype(BF16)
         return carry
 
     lax.fori_loop(0, n // ROWS, start, 0)
@@ -131,56 +169,77 @@
     lax.fori_loop(0, n // ROWS, scale, 0)
     transform(cols_ref, rows_ref)
 
-    def finish(b, carry):
+    def place(b, carry):
         at = pl.ds(pl.multiple_of(b * ROWS, ROWS), ROWS)
-        sums = [[None, None] for _ in range(modes)]
-        pad = jnp.zeros((8, n), F32)
-        beside = jnp.zeros((ROWS + 8, n), F32)
         for f in range(frames):
-            r, c = offsets[f]
+            r, tile, shift = offsets[f]
+            rows = pl.ds(r + b * ROWS, ROWS)
             at_f = pl.ds(pl.multiple_of(f * n + b * ROWS, ROWS), ROWS)
-            d_re = wide_ref[at_f, :n] - exit_ref[f, 0, at, :]
-            d_im = wide_ref[at_f, n:] - exit_ref[f, 1, at, :]
-            p_re = probe_ref[f, 0, at, :]
-            p_im = probe_ref[f, 1, at, :]
-            updates = (
-                p_re * d_re + p_im * d_im,
-                p_re * d_im - p_im * d_re,
-                p_re * p_re + p_im * p_im,
-            )
+            parts = [[], [], []]
+            for lane in range(lanes):
+                col = slice(lane * 128, lane * 128 + 128)
+                col_im = slice(n + lane * 128, n + lane * 128 + 128)
+                d_re = wide_ref[at_f, col] - exit_ref[f, 0, at, col]
+                d_im = wide_ref[at_f, col_im] - exit_ref[f, 1, at, col]
+                wide_ref[at_f, col] = d_re
+                wide_ref[at_f, col_im] = d_im
+                p_re = probe_ref[f, 0, at, col]
+                p_im = probe_ref[f, 1, at, col]
+                parts[0].append(pltpu.roll(p_re * d_re + p_im * d_im, shift, 1))
+                parts[1].append(pltpu.roll(p_re * d_im - p_im * d_re, shift, 1))
+                parts[2].append(pltpu.roll(p_re * p_re + p_im * p_im, shift, 1))
             for q in range(3):
-                placed = pltpu.roll(jnp.concatenate([updates[q], pad], 0), r & 7, 0)
-                placed = pltpu.roll(jnp.concatenate([placed, beside], 1), c, 1)
-                rows = pl.ds(pl.multiple_of((r >> 3) * 8 + b * ROWS, 8), ROWS + 8)
-                tot_ref[q, rows, :] = tot_ref[q, rows, :] + placed
-            o_re = grads_ref[f, 0, at, :]
-            o_im = grads_ref[f, 1, at, :]
-            g_re = o_re * d_re + o_im * d_im
-            g_im = o_re * d_im - o_im * d_re
-            grads_ref[f, 0, at, :] = g_re
-            grads_ref[f, 1, at, :] = g_im
-            for k in range(modes):
-                for q, g in ((0, g_re), (1, g_im)):
-                    term = weights[f][k] * g
-                    sums[k][q] = term if f == 0 else sums[k][q] + term
-        for k in range(modes):
-            keep = jnp.where(is_first, sums[k][0], sums[k][1])
-            give = jnp.where(is_first, sums[k][1], sums[k][0])
-            for i in range(ROWS // 8):
-                for j in range(n // 128):
-                    tile = b * (ROWS // 8 * (n // 128)) + i * (n // 128) + j
-                    keep_ref[tile, k] = keep[8 * i : 8 * i + 8, 128 * j : 128 * j + 128]
-                    give_ref[tile, k] = give[8 * i : 8 * i + 8, 128 * j : 128 * j + 128]
+                for t in range(lanes + 1):
+                    before = parts[q][t - 1] if t > 0 else 0.0
+                    after = parts[q][t] if t < lanes else 0.0
+                    value = jnp.where(column < shift, before, after)
+                    tot_ref[q, tile + t, rows, :] = tot_ref[q, tile + t, rows, :] + value
         return carry
 
-    lax.fori_loop(0, n // ROWS, finish, 0)
+    lax.fori_loop(0, n // ROWS, place, 0)
     stores = []
     for i, (dst, a, b) in enumerate(
-        ((t_own_ref, 0, 0), (t_right_ref, 0, n), (t_below_ref, n, 0), (t_corner_ref, n, n))
+        ((t_corner_ref, n, lanes), (t_right_ref, 0, lanes), (t_below_ref, n, 0), (t_own_ref, 0, 0))
     ):
-        stores.append(pltpu.make_async_copy(tot_ref.at[:, a : a + n, b : b + n], dst, out_sem.at[i]))
+        for lane in range(lanes):
+            stores.append(
+                pltpu.make_async_copy(
+                    quarter(tot_ref, a, b, lane), strip(dst, lane), out_sem.at[i * lanes + lane]
+                )
+            )
     for store in stores:
         store.start()
+
+    def finish(b, carry):
+        at = pl.ds(pl.multiple_of(b * 16, 16), 16)
+        for lane in range(lanes):
+            col = slice(lane * 128, lane * 128 + 128)
+            col_im = slice(n + lane * 128, n + lane * 128 + 128)
+            slopes = []
+            for f in range(frames):
+                at_f = pl.ds(pl.multiple_of(f * n + b * 16, 16), 16)
+                d_re = wide_ref[at_f, col]
+                d_im = wide_ref[at_f, col_im]
+                o_re = grads_ref[f, 0, at, col]
+                o_im = grads_ref[f, 1, at, col]
+                g_re = o_re * d_re + o_im * d_im
+                g_im = o_re * d_im - o_im * d_re
+                grads_ref[f, 0, at, col] = g_re
+                grads_ref[f, 1, at, col] = g_im
+                slopes.append((jnp.where(is_first, g_re, g_im), jnp.where(is_first, g_im, g_re)))
+            for k in range(modes):
+                keep = weights[0][k] * slopes[0][0]
+                give = weights[0][k] * slopes[0][1]
+                for f in range(1, frames):
+                    keep = keep + weights[f][k] * slopes[f][0]
+                    give = give + weights[f][k] * slopes[f][1]
+                for i in range(2):
+                    tile = (2 * b + i) * lanes + lane
+                    keep_ref[tile, k] = keep[8 * i : 8 * i + 8]
+                    give_ref[tile, k] = give[8 * i : 8 * i + 8]
+        return carry
+
+    lax.fori_loop(0, n // 16, finish, 0)
     for store in stores:
         store.wait()
 
@@ -197,11 +256,11 @@
     return pl.pallas_call(
         frames_kernel,
         out_shape=(piece, piece, jax.ShapeDtypeStruct((frames, 2, n, n), F32)) + (quarter,) * 4,
-        in_specs=[smem] * 4 + [hbm] * 4 + [vmem] * 4,
+        in_specs=[smem] * 4 + [hbm] * 5 + [vmem] * 4,
         out_specs=(vmem,) * 3 + (hbm,) * 4,
         scratch_shapes=[
-            pltpu.VMEM((2, 2 * n, 2 * n), F32),
-            pltpu.VMEM((3, 2 * n, 2 * n), F32),
+            pltpu.VMEM((2, 2 * n // 128, 2 * n, 128), F32),
+            pltpu.VMEM((3, 2 * n // 128, 2 * n, 128), F32),
             pltpu.VMEM((frames, 2, n, n), F32),
             pltpu.VMEM((frames, 2, n, n), F32),
             pltpu.VMEM((2 * n, 2 * n), BF16),
@@ -209,8 +268,8 @@
             pltpu.VMEM((2 * n, frames * n), BF16),
             pltpu.VMEM((frames * n, 2 * n), BF16),
             pltpu.VMEM((frames * n, 2 * n), F32),
-            pltpu.SemaphoreType.DMA((4,)),
-            pltpu.SemaphoreType.DMA((4,)),
+            pltpu.SemaphoreType.DMA((4 * n // 128,)),
+            pltpu.SemaphoreType.DMA((4 * n // 128,)),
         ],
         name="frames",
     )(core, positions, count, coefficients, *blocks, amplitudes, modes, *tables)
@@ -350,11 +409,12 @@
     )(core, count, coefficients, mine, other, old, grads)
 
 
-def moves(scans, cols, down, over):
+def moves(scans, cols, down, over, odd_from=None):
     pairs = []
     for s in range(scans):
         for c in range(cols):
-            if 0 <= s + down < scans and 0 <= c + over < cols:
+            inside = 0 <= s + down < scans and 0 <= c + over < cols
+            if inside and (odd_from is None or s % 2 == odd_from):
                 pairs.append((s * cols + c, (s + down) * cols + c + over))
     return pairs
 
@@ -368,10 +428,11 @@
     swap = [(0, 1), (1, 0)]
 
     def widen(block):
-        corner = lax.ppermute(block, ALL, moves(scans, cols, -1, -1))
         right = lax.ppermute(block, ALL, moves(scans, cols, 0, -1))
+        corner = lax.ppermute(block, ALL, moves(scans, cols, -1, -1, 0))
         below = lax.ppermute(block, ALL, moves(scans, cols, -1, 0))
-        return [block, right, below, corner]
+        beyond = lax.ppermute(right, "core", [(1, 0)])
+        return [block, right, below, corner, beyond]
 
     tables = make_tables(length)
     blocks = widen(object_field)
@@ -379,9 +440,10 @@
         keep, give, grads, t_own, t_right, t_below, t_corner = run_frames(
             core, positions, frame_count, coefficients, blocks, amplitudes, probe_modes, tables
         )
+        joined = t_right + lax.ppermute(t_corner, "core", [(0, 1)])
         kept = keep + lax.ppermute(give, "core", swap)
-        crossed = lax.ppermute(t_corner, ALL, moves(scans, cols, 1, 1))
-        arrived = lax.ppermute(t_right, ALL, moves(scans, cols, 0, 1))
+        arrived = lax.ppermute(joined, ALL, moves(scans, cols, 0, 1))
+        crossed = lax.ppermute(t_corner, ALL, moves(scans, cols, 1, 1, 1))
         lowered = lax.ppermute(t_below, ALL, moves(scans, cols, 1, 0))
         got = lax.all_to_all(kept, CHIPS, split_axis=0, concat_axis=0, tiled=True)
         settled = t_own + arrived + lowered + crossed

time: 255 us -> 248 us (0.973)
  the two profiles are of different devices: /device:TPU:25 before, /device:TPU:1 now
where the time goes in v1:
time: 248 us; the launch traced here: 246 us
  waiting for transfers between devices  97.5 us (39%)
  starting transfers between devices  69.4 us (28%)
  Pallas kernels  39 us (16%)
  blocking collectives  22 us (9%)
  other arithmetic  11.4 us (5%)
  local copies, waits for them, and re-layouts  5.07 us (2%)
    ppermute x2, waiting for transfers between devices, widen(): right = lax.ppermute(block, ALL, moves(scans, cols, 0, -1))  32.1 us
    ppermute x2, waiting for transfers between devices, on_device(): arrived = lax.ppermute(joined, ALL, moves(scans, cols, 0, 1))  28.4 us
    all_to_all x2, waiting for transfers between devices, on_device(): got = lax.all_to_all(kept, CHIPS, split_axis=0, concat_axis=0, tiled=True)  22.6 us
    all_to_all x1, blocking collectives, on_device(): lax.all_to_all(spread, CHIPS, split_axis=0, concat_axis=0, tiled=True)  22 us
    pallas_call x2, Pallas kernels, run_frames(): pl.pallas_call(frames_kernel, out_shape=(piece, piece, jax.ShapeDtypeStru...  20.8 us
    pallas_call x2, Pallas kernels, run_modes(): pl.pallas_call(functools.partial(modes_kernel, root_total=root_total), ou...  13.4 us
    all_to_all x2, starting transfers between devices, on_device(): got = lax.all_to_all(kept, CHIPS, split_axis=0, concat_axis=0, tiled=True)  12.8 us
    ppermute x2, starting transfers between devices, on_device(): crossed = lax.ppermute(t_corner, ALL, moves(scans, cols, 1, 1, 1))  11 us
  transfers between devices with their start and end apart: 23, of which 10 were waited for; matrix products, arithmetic and copies ran while one was open for 4% of the time, Pallas kernels for 4%

profile of v1, /device:TPU:1, one launch (start us, length us, event | category | flops | bytes accessed | tf_op | source)
XLA Modules:
  0.0 246.0 jit_solution(10740915167146705203)
XLA Ops:
  0.6 1.3 collective-permute-start
  1.9 1.3 collective-permute-start.2
  3.2 2.7 %collective-permute-start.1 = (f32[2,256,256]{2,1,0:T(8,128)}, f32[2,256,256]{2,1,0:T(8,128)S(1)}, u32[]{:S(2)}, u32[]{:S(2)}) collective-permute-start(f32[2,256,256]{2,1,0:T(8,128)} %own_ref.1), channel_id=1, source_target_pairs={{4,0},{5,1},{6,2},{7,3},{8,4},{9,5},{10,6},{11,7},{12,8},{13,9},{1... | collective-permute-start | bytes 1572872 | tf_op jit(solution)/shard_map/ppermute | solution.py:433
  5.9 15.8 %collective-permute-done.right_ref = f32[2,256,256]{2,1,0:T(8,128)S(1)} collective-permute-done((f32[2,256,256]{2,1,0:T(8,128)}, f32[2,256,256]{2,1,0:T(8,128)S(1)}, u32[]{:S(2)}, u32[]{:S(2)}) %collective-permute-start) | collective-permute-done | bytes 524320 | tf_op jit(solution)/shard_map/ppermute | solution.py:431
  21.8 3.5 %collective-permute-start.3 = (f32[2,256,256]{2,1,0:T(8,128)S(1)}, f32[2,256,256]{2,1,0:T(8,128)S(1)}, u32[]{:S(2)}, u32[]{:S(2)}) collective-permute-start(f32[2,256,256]{2,1,0:T(8,128)S(1)} %collective-permute-done.right_ref), channel_id=1, source_target_pairs={{4,0},{5,1},{6,2},{7,3},{12,8},{13,9},{14,10},{15,11},{20,16},{21,... | collective-permute-start | bytes 1572872 | tf_op jit(solution)/shard_map/ppermute | solution.py:434
  25.9 1.8 multiply_convert_fusion
  27.7 0.0 collective-permute-done.1.below_ref
  27.7 0.0 collective-permute-done.3.beyond_ref
  27.8 0.8 copy-done.14
  28.5 0.2 copy-done.15
  28.7 0.2 copy-done.16
  28.9 10.4 %frames.2 = (f32[64,4,8,128]{3,2,1,0:T(8,128)}, f32[64,4,8,128]{3,2,1,0:T(8,128)}, f32[2,2,256,256]{3,2,1,0:T(8,128)}, f32[3,256,256]{2,1,0:T(8,128)}, f32[3,256...) custom-call(s32[1]{0:T(128)} %bitcast.core_ref, s32[2,2]{1,0:T(2,128)} %pos_ref.3, ...), custom_call_target="tpu_custom_call" | custom-call | tf_op jit(solution)/shard_map/frames/pallas_call | solution.py:256
  39.3 0.0 copy-start.7
  39.3 1.4 collective-permute-start.5
  40.7 1.3 collective-permute-start.4
  42.0 4.2 %collective-permute-start.8 = (f32[3,256,256]{2,1,0:T(8,128)}, f32[3,256,256]{2,1,0:T(8,128)S(1)}, u32[]{:S(2)}, u32[]{:S(2)}) collective-permute-start(f32[3,256,256]{2,1,0:T(8,128)} %get-tuple-element.27), channel_id=1, source_target_pairs={{4,9},{5,10},{6,11},{12,17},{13,18},{14,19},{20,25},{21,26},{22,27... | collective-permute-start | bytes 2359304 | tf_op jit(solution)/shard_map/ppermute | solution.py:446
  46.2 1.9 collective-permute-start.7
  48.1 0.0 collective-permute-done.5
  48.1 1.2 add.58
  49.4 4.1 %collective-permute-start.6 = (f32[3,256,256]{2,1,0:T(8,128)S(1)}, f32[3,256,256]{2,1,0:T(8,128)}, u32[]{:S(2)}, u32[]{:S(2)}) collective-permute-start(f32[3,256,256]{2,1,0:T(8,128)S(1)} %add.58), channel_id=1, source_target_pairs={{0,1},{1,2},{2,3},{4,5},{5,6},{6,7},{8,9},{9,10},{10,11},{12,13},{... | collective-permute-start | bytes 2359304 | tf_op jit(solution)/shard_map/ppermute | solution.py:445
  53.5 0.0 collective-permute-done.4
  53.5 1.2 add.57
  54.7 8.2 %all-to-all-start = ((f32[64,4,8,128]{3,2,1,0:T(8,128)}), f32[64,4,8,128]{3,2,1,0:T(8,128)S(1)}, u32[]{:S(2)}, u32[]{:S(2)}) async-start(f32[64,4,8,128]{3,2,1,0:T(8,128)} %add.57), calls=%async_computation | async-start | bytes 2097152 | tf_op jit(solution)/shard_map/all_to_all | solution.py:448
  62.9 1.0 collective-permute-done.7
  63.9 19.1 %collective-permute-done.6 = f32[3,256,256]{2,1,0:T(8,128)} collective-permute-done((f32[3,256,256]{2,1,0:T(8,128)S(1)}, f32[3,256,256]{2,1,0:T(8,128)}, u32[]{:S(2)}, u32[]{:S(2)}) %collective-permute-start.6) | collective-permute-done | bytes 786464 | tf_op jit(solution)/shard_map/ppermute | solution.py:445
  83.0 1.6 add_add_fusion.1
  84.7 0.1 fusion.1.own_ref
  84.8 0.0 copy-start
  84.8 6.1 %all-to-all-done.got_ref = f32[64,4,8,128]{3,2,1,0:T(8,128)S(1)} async-done(((f32[64,4,8,128]{3,2,1,0:T(8,128)}), f32[64,4,8,128]{3,2,1,0:T(8,128)S(1)}, u32[]{:S(2)}, u32[]{:S(2)}) %all-to-all-start) | async-done | bytes 1048608 | tf_op jit(solution)/shard_map/all_to_all | solution.py:448
  90.9 1.0 copy-done.4
  91.9 2.4 spread.2
  94.3 22.0 %all_to_all.20.mine_ref = f32[64,4,8,128]{3,2,1,0:T(8,128)S(1)} all-to-all(f32[64,4,8,128]{3,2,1,0:T(8,128)} %spread.2), channel_id=1, replica_groups=mesh['z'=4,'x'=4,'core'=2,'y'=4] {'z','x','y'}, dimensions={0} | all-to-all | bytes 2097152 | tf_op jit(solution)/shard_map/all_to_all | solution.py:455
  116.3 2.4 collective-permute-start.9
  118.7 1.3 collective-permute-start.10
  120.0 1.3 collective-permute-start.12
  121.3 2.1 collective-permute-start.11
  123.4 16.3 %collective-permute-done.10.right_ref = f32[2,256,256]{2,1,0:T(8,128)S(1)} collective-permute-done((f32[2,256,256]{2,1,0:T(8,128)S(1)}, f32[2,256,256]{2,1,0:T(8,128)S(1)}, u32[]{:S(2)}, u32[]{:S(2)}) %collective-permute-start.10) | collective-permute-done | bytes 524320 | tf_op jit(solution)/shard_map/ppermute | solution.py:431
  139.7 3.6 %collective-permute-start.13 = (f32[2,256,256]{2,1,0:T(8,128)S(1)}, f32[2,256,256]{2,1,0:T(8,128)}, u32[]{:S(2)}, u32[]{:S(2)}) collective-permute-start(f32[2,256,256]{2,1,0:T(8,128)S(1)} %collective-permute-done.10.right_ref), channel_id=1, source_target_pairs={{4,0},{5,1},{6,2},{7,3},{12,8},{13,9},{14,10},{15,11},{20,16},{21,... | collective-permute-start | bytes 1572872 | tf_op jit(solution)/shard_map/ppermute | solution.py:434
  143.2 0.0 collective-permute-done.9.other_ref
  143.2 1.0 copy-done.9
  144.2 6.7 %modes.2 = (f32[4,2,256,256]{3,2,1,0:T(8,128)}, f32[2,4]{1,0:T(2,128)}) custom-call(s32[1]{0:T(128)} %bitcast.core_ref, s32[1]{0:T(128)S(6)} %copy.9.cnt_ref, f32[2,4]{1,0:T(2,128)} %coef_ref.3, f32[64,4,8,128]{3,2,1,0:T(8,128)} %copy-done.3, f32[64,4,8,128]{3,2,1,0:T(8,128)} %copy-done.9, f32[4,2,256,256]{3,2,1,0:T(8,128)} %old_ref.1, ...), custom_call_target="tpu_custom_call" | custom-call | tf_op jit(solution)/shard_map/modes/pallas_call | solution.py:399
  150.9 0.0 collective-permute-done.12.corner_ref
  151.0 10.4 %frames.3 = (f32[64,4,8,128]{3,2,1,0:T(8,128)}, f32[64,4,8,128]{3,2,1,0:T(8,128)}, f32[2,2,256,256]{3,2,1,0:T(8,128)}, f32[3,256,256]{2,1,0:T(8,128)}, f32[3,256...) custom-call(s32[1]{0:T(128)} %bitcast.core_ref, s32[2,2]{1,0:T(2,128)} %pos_ref.3, ...), custom_call_target="tpu_custom_call" | custom-call | tf_op jit(solution)/shard_map/frames/pallas_call | solution.py:256
  161.4 0.1 collective-permute-start.18
  161.5 2.9 %collective-permute-done.18 = f32[64,4,8,128]{3,2,1,0:T(8,128)S(1)} collective-permute-done((f32[64,4,8,128]{3,2,1,0:T(8,128)}, f32[64,4,8,128]{3,2,1,0:T(8,128)S(1)}, u32[]{:S(2)}, u32[]{:S(2)}) %collective-permute-start.18) | collective-permute-done | bytes 1048608 | tf_op jit(solution)/shard_map/ppermute | solution.py:444
  164.3 2.4 add.70
  166.7 4.7 %all-to-all-start.2 = ((f32[64,4,8,128]{3,2,1,0:T(8,128)}), f32[64,4,8,128]{3,2,1,0:T(8,128)S(1)}, u32[]{:S(2)}, u32[]{:S(2)}) async-start(f32[64,4,8,128]{3,2,1,0:T(8,128)} %add.70), calls=%async_computation.2 | async-start | bytes 2097152 | tf_op jit(solution)/shard_map/all_to_all | solution.py:448
  171.4 1.4 collective-permute-start.14
  172.8 16.4 %all-to-all-done.2.got_ref = f32[64,4,8,128]{3,2,1,0:T(8,128)S(1)} async-done(((f32[64,4,8,128]{3,2,1,0:T(8,128)}), f32[64,4,8,128]{3,2,1,0:T(8,128)S(1)}, u32[]{:S(2)}, u32[]{:S(2)}) %all-to-all-start.2) | async-done | bytes 1048608 | tf_op jit(solution)/shard_map/all_to_all | solution.py:448
  189.3 1.0 copy-done.5
  190.2 2.4 spread.3
  192.6 4.9 %all-to-all-start.3 = ((f32[64,4,8,128]{3,2,1,0:T(8,128)}), f32[64,4,8,128]{3,2,1,0:T(8,128)S(1)}, u32[]{:S(2)}, u32[]{:S(2)}) async-start(f32[64,4,8,128]{3,2,1,0:T(8,128)} %spread.3), calls=%async_computation.3 | async-start | bytes 2097152 | tf_op jit(solution)/shard_map/all_to_all | solution.py:455
  197.6 6.7 %collective-permute-start.17 = (f32[3,256,256]{2,1,0:T(8,128)}, f32[3,256,256]{2,1,0:T(8,128)}, u32[]{:S(2)}, u32[]{:S(2)}) collective-permute-start(f32[3,256,256]{2,1,0:T(8,128)} %get-tuple-element.36), channel_id=1, source_target_pairs={{4,9},{5,10},{6,11},{12,17},{13,18},{14,19},{20,25},{21,26},{22,27... | collective-permute-start | bytes 2359304 | tf_op jit(solution)/shard_map/ppermute | solution.py:446
  204.3 1.9 collective-permute-start.16
  206.2 0.1 add.64
  206.3 4.0 %collective-permute-start.15 = (f32[3,256,256]{2,1,0:T(8,128)S(1)}, f32[3,256,256]{2,1,0:T(8,128)}, u32[]{:S(2)}, u32[]{:S(2)}) collective-permute-start(f32[3,256,256]{2,1,0:T(8,128)S(1)} %add.64), channel_id=1, source_target_pairs={{0,1},{1,2},{2,3},{4,5},{5,6},{6,7},{8,9},{9,10},{10,11},{12,13},{... | collective-permute-start | bytes 2359304 | tf_op jit(solution)/shard_map/ppermute | solution.py:445
  210.3 3.7 %all-to-all-done.3.mine_ref = f32[64,4,8,128]{3,2,1,0:T(8,128)S(1)} async-done(((f32[64,4,8,128]{3,2,1,0:T(8,128)}), f32[64,4,8,128]{3,2,1,0:T(8,128)S(1)}, u32[]{:S(2)}, u32[]{:S(2)}) %all-to-all-start.3) | async-done | bytes 1048608 | tf_op jit(solution)/shard_map/all_to_all | solution.py:455
  213.9 5.2 %collective-permute-start.19 = (f32[64,4,8,128]{3,2,1,0:T(8,128)S(1)}, f32[64,4,8,128]{3,2,1,0:T(8,128)S(1)}, u32[]{:S(2)}, u32[]{:S(2)}) collective-permute-start(f32[64,4,8,128]{3,2,1,0:T(8,128)S(1)} %all-to-all-done.3.mine_ref), channel_id=1, source_target_pairs={{0,4},{4,0},{1,5},{5,1},{2,6},{6,2},{3,7},{7,3},{8,12},{12,8},{9,1... | collective-permute-start | bytes 3145736 | tf_op jit(solution)/shard_map/ppermute | solution.py:456
  219.1 6.9 %collective-permute-done.16 = f32[3,256,256]{2,1,0:T(8,128)} collective-permute-done((f32[3,256,256]{2,1,0:T(8,128)}, f32[3,256,256]{2,1,0:T(8,128)}, u32[]{:S(2)}, u32[]{:S(2)}) %collective-permute-start.16) | collective-permute-done | bytes 786464 | tf_op jit(solution)/shard_map/ppermute | solution.py:447
  226.0 9.3 %collective-permute-done.15 = f32[3,256,256]{2,1,0:T(8,128)} collective-permute-done((f32[3,256,256]{2,1,0:T(8,128)S(1)}, f32[3,256,256]{2,1,0:T(8,128)}, u32[]{:S(2)}, u32[]{:S(2)}) %collective-permute-start.15) | collective-permute-done | bytes 786464 | tf_op jit(solution)/shard_map/ppermute | solution.py:445
  235.3 2.1 add_add_fusion
  237.5 0.9 fusion
  238.4 1.0 copy-done.8
  239.3 6.7 %modes.3 = (f32[4,2,256,256]{3,2,1,0:T(8,128)}, f32[2,4]{1,0:T(2,128)}) custom-call(s32[1]{0:T(128)} %bitcast.core_ref, s32[1]{0:T(128)S(6)} %copy.9.cnt_ref, f32[2,4]{1,0:T(2,128)} %get-tuple-element.32.coef_ref, f32[64,4,8,128]{3,2,1,0:T(8,128)} %copy-done.2, f32[64,4,8,128]{3,2,1,0:T(8,128)} %copy-done.8, ...), custom_call_target="tpu_custom_call" | custom-call | tf_op jit(solution)/shard_map/modes/pallas_call | solution.py:399
  (34 shorter events, 0.1 us)
Async XLA Ops:
  0.6 21.1 %collective-permute-start = (f32[2,256,256]{2,1,0:T(8,128)}, f32[2,256,256]{2,1,0:T(8,128)S(1)}, u32[]{:S(2)}, u32[]{:S(2)}) collective-permute-start(f32[2,256,256]{2,1,0:T(8,128)} %own_ref.1), channel_id=1, source_target_pairs={{1,0},{2,1},{3,2},{5,4},{6,5},{7,6},{9,8},{10,9},{11,10},{13,12},{... | collective-permute-start | bytes 1572872 | tf_op jit(solution)/shard_map/ppermute | solution.py:431
  1.9 25.8 %collective-permute-start.2 = (f32[2,256,256]{2,1,0:T(8,128)}, f32[2,256,256]{2,1,0:T(8,128)S(1)}, u32[]{:S(2)}, u32[]{:S(2)}) collective-permute-start(f32[2,256,256]{2,1,0:T(8,128)} %own_ref.1), channel_id=1, source_target_pairs={{9,4},{10,5},{11,6},{17,12},{18,13},{19,14},{25,20},{26,21},{27,22... | collective-permute-start | bytes 1572872 | tf_op jit(solution)/shard_map/ppermute | solution.py:432
  3.2 24.5 %collective-permute-start.1 = (f32[2,256,256]{2,1,0:T(8,128)}, f32[2,256,256]{2,1,0:T(8,128)S(1)}, u32[]{:S(2)}, u32[]{:S(2)}) collective-permute-start(f32[2,256,256]{2,1,0:T(8,128)} %own_ref.1), channel_id=1, source_target_pairs={{4,0},{5,1},{6,2},{7,3},{8,4},{9,5},{10,6},{11,7},{12,8},{13,9},{1... | collective-permute-start | bytes 1572872 | tf_op jit(solution)/shard_map/ppermute | solution.py:433
  21.8 6.0 %copy-start.12 = (f32[2,256,256]{2,1,0:T(8,128)}, f32[2,256,256]{2,1,0:T(8,128)S(1)}, u32[]{:S(2)}) copy-start(f32[2,256,256]{2,1,0:T(8,128)S(1)} %collective-permute-done.right_ref) | copy-start | bytes 1572868
  21.8 5.9 %collective-permute-start.3 = (f32[2,256,256]{2,1,0:T(8,128)S(1)}, f32[2,256,256]{2,1,0:T(8,128)S(1)}, u32[]{:S(2)}, u32[]{:S(2)}) collective-permute-start(f32[2,256,256]{2,1,0:T(8,128)S(1)} %collective-permute-done.right_ref), channel_id=1, source_target_pairs={{4,0},{5,1},{6,2},{7,3},{12,8},{13,9},{14,10},{15,11},{20,16},{21,... | collective-permute-start | bytes 1572872 | tf_op jit(solution)/shard_map/ppermute | solution.py:434
  27.7 0.8 copy-start.14
  27.7 1.0 copy-start.15
  27.7 1.1 copy-start.16
  39.3 14.2 %copy-start.7 = (f32[64,4,8,128]{3,2,1,0:T(8,128)S(1)}, f32[64,4,8,128]{3,2,1,0:T(8,128)}, u32[]{:S(2)}) copy-start(f32[64,4,8,128]{3,2,1,0:T(8,128)} %get-tuple-element.23) | copy-start | bytes 3145732
  39.3 8.9 %collective-permute-start.5 = (f32[3,256,256]{2,1,0:T(8,128)}, f32[3,256,256]{2,1,0:T(8,128)S(1)}, u32[]{:S(2)}, u32[]{:S(2)}) collective-permute-start(f32[3,256,256]{2,1,0:T(8,128)} %get-tuple-element.27), channel_id=1, source_target_pairs={{0,4},{1,5},{2,6},{3,7},{8,12},{9,13},{10,14},{11,15},{16,20},{17,... | collective-permute-start | bytes 2359304 | tf_op jit(solution)/shard_map/ppermute | solution.py:443
  40.7 12.8 %collective-permute-start.4 = (f32[64,4,8,128]{3,2,1,0:T(8,128)}, f32[64,4,8,128]{3,2,1,0:T(8,128)S(1)}, u32[]{:S(2)}, u32[]{:S(2)}) collective-permute-start(f32[64,4,8,128]{3,2,1,0:T(8,128)} %get-tuple-element.24), channel_id=1, source_target_pairs={{0,4},{4,0},{1,5},{5,1},{2,6},{6,2},{3,7},{7,3},{8,12},{12,8},{9,1... | collective-permute-start | bytes 3145736 | tf_op jit(solution)/shard_map/ppermute | solution.py:444
  42.0 21.9 %collective-permute-start.8 = (f32[3,256,256]{2,1,0:T(8,128)}, f32[3,256,256]{2,1,0:T(8,128)S(1)}, u32[]{:S(2)}, u32[]{:S(2)}) collective-permute-start(f32[3,256,256]{2,1,0:T(8,128)} %get-tuple-element.27), channel_id=1, source_target_pairs={{4,9},{5,10},{6,11},{12,17},{13,18},{14,19},{20,25},{21,26},{22,27... | collective-permute-start | bytes 2359304 | tf_op jit(solution)/shard_map/ppermute | solution.py:446
  46.2 17.7 %collective-permute-start.7 = (f32[3,256,256]{2,1,0:T(8,128)}, f32[3,256,256]{2,1,0:T(8,128)}, u32[]{:S(2)}, u32[]{:S(2)}) collective-permute-start(f32[3,256,256]{2,1,0:T(8,128)} %get-tuple-element.28), channel_id=1, source_target_pairs={{0,4},{1,5},{2,6},{3,7},{4,8},{5,9},{6,10},{7,11},{8,12},{9,13},{1... | collective-permute-start | bytes 2359304 | tf_op jit(solution)/shard_map/ppermute | solution.py:447
  49.4 33.6 %collective-permute-start.6 = (f32[3,256,256]{2,1,0:T(8,128)S(1)}, f32[3,256,256]{2,1,0:T(8,128)}, u32[]{:S(2)}, u32[]{:S(2)}) collective-permute-start(f32[3,256,256]{2,1,0:T(8,128)S(1)} %add.58), channel_id=1, source_target_pairs={{0,1},{1,2},{2,3},{4,5},{5,6},{6,7},{8,9},{9,10},{10,11},{12,13},{... | collective-permute-start | bytes 2359304 | tf_op jit(solution)/shard_map/ppermute | solution.py:445
  53.5 29.5 %copy-start.11 = (f32[3,256,256]{2,1,0:T(8,128)S(1)}, f32[3,256,256]{2,1,0:T(8,128)}, u32[]{:S(2)}) copy-start(f32[3,256,256]{2,1,0:T(8,128)} %get-tuple-element.25) | copy-start | bytes 2359300
  54.7 36.2 %all-to-all-start = ((f32[64,4,8,128]{3,2,1,0:T(8,128)}), f32[64,4,8,128]{3,2,1,0:T(8,128)S(1)}, u32[]{:S(2)}, u32[]{:S(2)}) async-start(f32[64,4,8,128]{3,2,1,0:T(8,128)} %add.57), calls=%async_computation | async-start | bytes 2097152 | tf_op jit(solution)/shard_map/all_to_all | solution.py:448
  83.0 1.7 copy-start.6
  84.8 36.5 %copy-start = (f32[2,256,256]{2,1,0:T(8,128)}, f32[2,256,256]{2,1,0:T(8,128)S(1)}, u32[]{:S(2)}) copy-start(f32[2,256,256]{2,1,0:T(8,128)S(1)} %fusion.1.own_ref) | copy-start | bytes 1572868
  90.9 1.0 copy-start.4
  116.3 26.9 %copy-start.3 = (f32[64,4,8,128]{3,2,1,0:T(8,128)}, f32[64,4,8,128]{3,2,1,0:T(8,128)S(1)}, u32[]{:S(2)}) copy-start(f32[64,4,8,128]{3,2,1,0:T(8,128)S(1)} %all_to_all.20.mine_ref) | copy-start | bytes 3145732
  116.3 26.9 %collective-permute-start.9 = (f32[64,4,8,128]{3,2,1,0:T(8,128)S(1)}, f32[64,4,8,128]{3,2,1,0:T(8,128)S(1)}, u32[]{:S(2)}, u32[]{:S(2)}) collective-permute-start(f32[64,4,8,128]{3,2,1,0:T(8,128)S(1)} %all_to_all.20.mine_ref), channel_id=1, source_target_pairs={{0,4},{4,0},{1,5},{5,1},{2,6},{6,2},{3,7},{7,3},{8,12},{12,8},{9,1... | collective-permute-start | bytes 3145736 | tf_op jit(solution)/shard_map/ppermute | solution.py:456
  118.7 21.0 %collective-permute-start.10 = (f32[2,256,256]{2,1,0:T(8,128)S(1)}, f32[2,256,256]{2,1,0:T(8,128)S(1)}, u32[]{:S(2)}, u32[]{:S(2)}) collective-permute-start(f32[2,256,256]{2,1,0:T(8,128)S(1)} %fusion.1.own_ref), channel_id=1, source_target_pairs={{1,0},{2,1},{3,2},{5,4},{6,5},{7,6},{9,8},{10,9},{11,10},{13,12},{... | collective-permute-start | bytes 1572872 | tf_op jit(solution)/shard_map/ppermute | solution.py:431
  120.0 31.0 %collective-permute-start.12 = (f32[2,256,256]{2,1,0:T(8,128)S(1)}, f32[2,256,256]{2,1,0:T(8,128)}, u32[]{:S(2)}, u32[]{:S(2)}) collective-permute-start(f32[2,256,256]{2,1,0:T(8,128)S(1)} %fusion.1.own_ref), channel_id=1, source_target_pairs={{9,4},{10,5},{11,6},{17,12},{18,13},{19,14},{25,20},{26,21},{27,22... | collective-permute-start | bytes 1572872 | tf_op jit(solution)/shard_map/ppermute | solution.py:432
  121.3 29.7 %collective-permute-start.11 = (f32[2,256,256]{2,1,0:T(8,128)S(1)}, f32[2,256,256]{2,1,0:T(8,128)}, u32[]{:S(2)}, u32[]{:S(2)}) collective-permute-start(f32[2,256,256]{2,1,0:T(8,128)S(1)} %fusion.1.own_ref), channel_id=1, source_target_pairs={{4,0},{5,1},{6,2},{7,3},{8,4},{9,5},{10,6},{11,7},{12,8},{13,9},{1... | collective-permute-start | bytes 1572872 | tf_op jit(solution)/shard_map/ppermute | solution.py:433
  139.7 11.3 %copy-start.13 = (f32[2,256,256]{2,1,0:T(8,128)}, f32[2,256,256]{2,1,0:T(8,128)S(1)}, u32[]{:S(2)}) copy-start(f32[2,256,256]{2,1,0:T(8,128)S(1)} %collective-permute-done.10.right_ref) | copy-start | bytes 1572868
  139.7 11.3 %collective-permute-start.13 = (f32[2,256,256]{2,1,0:T(8,128)S(1)}, f32[2,256,256]{2,1,0:T(8,128)}, u32[]{:S(2)}, u32[]{:S(2)}) collective-permute-start(f32[2,256,256]{2,1,0:T(8,128)S(1)} %collective-permute-done.10.right_ref), channel_id=1, source_target_pairs={{4,0},{5,1},{6,2},{7,3},{12,8},{13,9},{14,10},{15,11},{20,16},{21,... | collective-permute-start | bytes 1572872 | tf_op jit(solution)/shard_map/ppermute | solution.py:434
  143.2 1.0 copy-start.9
  161.4 3.0 %collective-permute-start.18 = (f32[64,4,8,128]{3,2,1,0:T(8,128)}, f32[64,4,8,128]{3,2,1,0:T(8,128)S(1)}, u32[]{:S(2)}, u32[]{:S(2)}) collective-permute-start(f32[64,4,8,128]{3,2,1,0:T(8,128)} %get-tuple-element.39), channel_id=1, source_target_pairs={{0,4},{4,0},{1,5},{5,1},{2,6},{6,2},{3,7},{7,3},{8,12},{12,8},{9,1... | collective-permute-start | bytes 3145736 | tf_op jit(solution)/shard_map/ppermute | solution.py:444
  166.7 22.5 %all-to-all-start.2 = ((f32[64,4,8,128]{3,2,1,0:T(8,128)}), f32[64,4,8,128]{3,2,1,0:T(8,128)S(1)}, u32[]{:S(2)}, u32[]{:S(2)}) async-start(f32[64,4,8,128]{3,2,1,0:T(8,128)} %add.70), calls=%async_computation.2 | async-start | bytes 2097152 | tf_op jit(solution)/shard_map/all_to_all | solution.py:448
  171.4 34.8 %copy-start.10 = (f32[3,256,256]{2,1,0:T(8,128)S(1)}, f32[3,256,256]{2,1,0:T(8,128)}, u32[]{:S(2)}) copy-start(f32[3,256,256]{2,1,0:T(8,128)} %get-tuple-element.35) | copy-start | bytes 2359300
  171.4 34.8 %collective-permute-start.14 = (f32[3,256,256]{2,1,0:T(8,128)}, f32[3,256,256]{2,1,0:T(8,128)S(1)}, u32[]{:S(2)}, u32[]{:S(2)}) collective-permute-start(f32[3,256,256]{2,1,0:T(8,128)} %get-tuple-element.36), channel_id=1, source_target_pairs={{0,4},{1,5},{2,6},{3,7},{8,12},{9,13},{10,14},{11,15},{16,20},{17,... | collective-permute-start | bytes 2359304 | tf_op jit(solution)/shard_map/ppermute | solution.py:443
  189.3 1.0 copy-start.5
  192.6 21.3 %all-to-all-start.3 = ((f32[64,4,8,128]{3,2,1,0:T(8,128)}), f32[64,4,8,128]{3,2,1,0:T(8,128)S(1)}, u32[]{:S(2)}, u32[]{:S(2)}) async-start(f32[64,4,8,128]{3,2,1,0:T(8,128)} %spread.3), calls=%async_computation.3 | async-start | bytes 2097152 | tf_op jit(solution)/shard_map/all_to_all | solution.py:455
  197.6 28.5 %collective-permute-start.17 = (f32[3,256,256]{2,1,0:T(8,128)}, f32[3,256,256]{2,1,0:T(8,128)}, u32[]{:S(2)}, u32[]{:S(2)}) collective-permute-start(f32[3,256,256]{2,1,0:T(8,128)} %get-tuple-element.36), channel_id=1, source_target_pairs={{4,9},{5,10},{6,11},{12,17},{13,18},{14,19},{20,25},{21,26},{22,27... | collective-permute-start | bytes 2359304 | tf_op jit(solution)/shard_map/ppermute | solution.py:446
  204.3 21.7 %collective-permute-start.16 = (f32[3,256,256]{2,1,0:T(8,128)}, f32[3,256,256]{2,1,0:T(8,128)}, u32[]{:S(2)}, u32[]{:S(2)}) collective-permute-start(f32[3,256,256]{2,1,0:T(8,128)} %get-tuple-element.37), channel_id=1, source_target_pairs={{0,4},{1,5},{2,6},{3,7},{4,8},{5,9},{6,10},{7,11},{8,12},{9,13},{1... | collective-permute-start | bytes 2359304 | tf_op jit(solution)/shard_map/ppermute | solution.py:447
  206.3 29.0 %collective-permute-start.15 = (f32[3,256,256]{2,1,0:T(8,128)S(1)}, f32[3,256,256]{2,1,0:T(8,128)}, u32[]{:S(2)}, u32[]{:S(2)}) collective-permute-start(f32[3,256,256]{2,1,0:T(8,128)S(1)} %add.64), channel_id=1, source_target_pairs={{0,1},{1,2},{2,3},{4,5},{5,6},{6,7},{8,9},{9,10},{10,11},{12,13},{... | collective-permute-start | bytes 2359304 | tf_op jit(solution)/shard_map/ppermute | solution.py:445
  213.9 23.5 %copy-start.2 = (f32[64,4,8,128]{3,2,1,0:T(8,128)}, f32[64,4,8,128]{3,2,1,0:T(8,128)S(1)}, u32[]{:S(2)}) copy-start(f32[64,4,8,128]{3,2,1,0:T(8,128)S(1)} %all-to-all-done.3.mine_ref) | copy-start | bytes 3145732
  213.9 24.4 %collective-permute-start.19 = (f32[64,4,8,128]{3,2,1,0:T(8,128)S(1)}, f32[64,4,8,128]{3,2,1,0:T(8,128)S(1)}, u32[]{:S(2)}, u32[]{:S(2)}) collective-permute-start(f32[64,4,8,128]{3,2,1,0:T(8,128)S(1)} %all-to-all-done.3.mine_ref), channel_id=1, source_target_pairs={{0,4},{4,0},{1,5},{5,1},{2,6},{6,2},{3,7},{7,3},{8,12},{12,8},{9,1... | collective-permute-start | bytes 3145736 | tf_op jit(solution)/shard_map/ppermute | solution.py:456
  235.3 2.1 copy-start.1
  238.3 1.0 copy-start.8

commit v2 on v1

--- a/solution.py
+++ b/solution.py
@@ -44,7 +44,7 @@
 
 
 def frames_kernel(
-    core_ref, pos_ref, cnt_ref, coef_ref, own_ref, right_ref, below_ref, corner_ref, beyond_ref,
+    core_ref, pos_ref, cnt_ref, coef_ref, own_ref, right_ref, below_ref, corner_ref,
     amp_ref, modes_ref, cos_ref, sin_ref,
     keep_ref, give_ref, grads_ref, t_own_ref, t_right_ref, t_below_ref, t_corner_ref,
     ext_ref, tot_ref, probe_ref, exit_ref, rows_ref, cols_ref, stack_ref, side_ref, wide_ref,
@@ -67,20 +67,10 @@
             for lane in range(lanes)
         ]
 
-    loads = load(0, own_ref, 0, 0) + load(1, right_ref, 0, lanes) + load(2, below_ref, n, 0)
+    loads = load(0, own_ref, 0, 0) + load(1, right_ref, 0, lanes)
+    loads += load(2, below_ref, n, 0) + load(3, corner_ref, n, lanes)
     for copy in loads:
         copy.start()
-
-    @pl.when(is_first)
-    def _():
-        for copy in load(3, beyond_ref, n, lanes):
-            copy.start()
-
-    @pl.when(jnp.logical_not(is_first))
-    def _():
-        for copy in load(3, corner_ref, n, lanes):
-            copy.start()
-
     fill_tables(cos_ref, sin_ref, rows_ref, cols_ref)
 
     def clear(t, carry):
@@ -99,7 +89,7 @@
         [jnp.where(f < cnt_ref[0], coef_ref[f, k], 0.0) for k in range(modes)] for f in range(frames)
     ]
     column = lax.broadcasted_iota(jnp.int32, (ROWS, 128), 1)
-    for copy in loads + load(3, corner_ref, n, lanes):
+    for copy in loads:
         copy.wait()
 
     def patch_rows(f, plane, b):
@@ -256,7 +246,7 @@
     return pl.pallas_call(
         frames_kernel,
         out_shape=(piece, piece, jax.ShapeDtypeStruct((frames, 2, n, n), F32)) + (quarter,) * 4,
-        in_specs=[smem] * 4 + [hbm] * 5 + [vmem] * 4,
+        in_specs=[smem] * 4 + [hbm] * 4 + [vmem] * 4,
         out_specs=(vmem,) * 3 + (hbm,) * 4,
         scratch_shapes=[
             pltpu.VMEM((2, 2 * n // 128, 2 * n, 128), F32),
@@ -409,12 +399,11 @@
     )(core, count, coefficients, mine, other, old, grads)
 
 
-def moves(scans, cols, down, over, odd_from=None):
+def moves(scans, cols, down, over):
     pairs = []
     for s in range(scans):
         for c in range(cols):
-            inside = 0 <= s + down < scans and 0 <= c + over < cols
-            if inside and (odd_from is None or s % 2 == odd_from):
+            if 0 <= s + down < scans and 0 <= c + over < cols:
                 pairs.append((s * cols + c, (s + down) * cols + c + over))
     return pairs
 
@@ -429,28 +418,26 @@
 
     def widen(block):
         right = lax.ppermute(block, ALL, moves(scans, cols, 0, -1))
-        corner = lax.ppermute(block, ALL, moves(scans, cols, -1, -1, 0))
         below = lax.ppermute(block, ALL, moves(scans, cols, -1, 0))
-        beyond = lax.ppermute(right, "core", [(1, 0)])
-        return [block, right, below, corner, beyond]
-
-    tables = make_tables(length)
+        corner = lax.ppermute(right, ALL, moves(scans, cols, -1, 0))
+        return [block, right, below, corner]
+
+    tables = lax.optimization_barrier(make_tables(length))
     blocks = widen(object_field)
     for iteration in range(ITERS):
         keep, give, grads, t_own, t_right, t_below, t_corner = run_frames(
             core, positions, frame_count, coefficients, blocks, amplitudes, probe_modes, tables
         )
-        joined = t_right + lax.ppermute(t_corner, "core", [(0, 1)])
+        crossed = lax.ppermute(t_corner, ALL, moves(scans, cols, 1, 0))
+        joined = t_right + crossed
         kept = keep + lax.ppermute(give, "core", swap)
         arrived = lax.ppermute(joined, ALL, moves(scans, cols, 0, 1))
-        crossed = lax.ppermute(t_corner, ALL, moves(scans, cols, 1, 1, 1))
         lowered = lax.ppermute(t_below, ALL, moves(scans, cols, 1, 0))
         got = lax.all_to_all(kept, CHIPS, split_axis=0, concat_axis=0, tiled=True)
-        settled = t_own + arrived + lowered + crossed
+        settled = t_own + arrived + lowered
         object_field = object_field + settled[:2] / (settled[2] + 1.0)
         if iteration + 1 < ITERS:
             blocks = widen(object_field)
-            got, object_field = lax.optimization_barrier((got, object_field))
         spread = run_spread(got)
         mine = lax.all_to_all(spread, CHIPS, split_axis=0, concat_axis=0, tiled=True)
         other = lax.ppermute(mine, "core", swap)

time: 248 us -> 220 us (0.89)
  blocking collectives: 22 us -> 0 us
  waiting for transfers between devices: 97.5 us -> 84.7 us
  starting transfers between devices: 69.4 us -> 73.1 us
  other arithmetic: 11.4 us -> 14 us
    all_to_all x1 -> x0, blocking collectives: 22 us -> none  [on_device(): lax.all_to_all(spread, CHIPS, split_axis=0, concat_axis=0, tiled=True)]
    ppermute x2, waiting for transfers between devices: 28.4 us -> 9.7 us  [on_device(): arrived = lax.ppermute(joined, ALL, moves(scans, cols, 0, 1))]
    all_to_all x1 -> x2, waiting for transfers between devices: 3.66 us -> 19.6 us  [on_device(): lax.all_to_all(spread, CHIPS, split_axis=0, concat_axis=0, tiled=True)]
    ppermute x8 -> x4, starting transfers between devices: 23.5 us -> 13.4 us  [the longest x2 7.12 us: on_device(): crossed = lax.ppermute(t_corner, ALL, moves(scans, cols, 1, 0))]
    ppermute x2, waiting for transfers between devices: 32.1 us -> 23.1 us  [widen(): right = lax.ppermute(block, ALL, moves(scans, cols, 0, -1))]
    ppermute x2, waiting for transfers between devices: 7.86 us -> 0.01 us  [on_device(): lowered = lax.ppermute(t_below, ALL, moves(scans, cols, 1, 0))]
    ppermute x8 -> x4, waiting for transfers between devices: 0.02 us -> 5.7 us  [the longest x2 5.7 us: widen(): corner = lax.ppermute(right, ALL, moves(scans, cols, -1, 0))]
    all_to_all x2, starting transfers between devices: 12.8 us -> 18.2 us  [on_device(): got = lax.all_to_all(kept, CHIPS, split_axis=0, concat_axis=0, tiled=True)]
  transfers between devices with their start and end apart: 23 -> 20, of which waited for: 10 -> 10; matrix products, arithmetic and copies ran while one was open for 4% -> 5% of each run, Pallas kernels for 4% -> 5%
where the time goes in v2:
time: 220 us; the launch traced here: 218 us
  waiting for transfers between devices  84.7 us (38%)
  starting transfers between devices  73.1 us (33%)
  Pallas kernels  39 us (18%)
  other arithmetic  14 us (6%)
  local copies, waits for them, and re-layouts  5.8 us (3%)
    all_to_all x2, waiting for transfers between devices, on_device(): got = lax.all_to_all(kept, CHIPS, split_axis=0, concat_axis=0, tiled=True)  23.8 us
    ppermute x2, waiting for transfers between devices, widen(): right = lax.ppermute(block, ALL, moves(scans, cols, 0, -1))  23.1 us
    pallas_call x2, Pallas kernels, run_frames(): pl.pallas_call(frames_kernel, out_shape=(piece, piece, jax.ShapeDtypeStru...  20.8 us
    all_to_all x2, waiting for transfers between devices, on_device(): lax.all_to_all(spread, CHIPS, split_axis=0, concat_axis=0, tiled=True)  19.6 us
    all_to_all x2, starting transfers between devices, on_device(): got = lax.all_to_all(kept, CHIPS, split_axis=0, concat_axis=0, tiled=True)  18.2 us
    pallas_call x2, Pallas kernels, run_modes(): pl.pallas_call(functools.partial(modes_kernel, root_total=root_total), ou...  13.4 us
    all_to_all x2, starting transfers between devices, on_device(): lax.all_to_all(spread, CHIPS, split_axis=0, concat_axis=0, tiled=True)  9.87 us
    ppermute x2, waiting for transfers between devices, on_device(): arrived = lax.ppermute(joined, ALL, moves(scans, cols, 0, 1))  9.7 us
  transfers between devices with their start and end apart: 20, of which 10 were waited for; matrix products, arithmetic and copies ran while one was open for 5% of the time, Pallas kernels for 5%

profile of v2, /device:TPU:1, one launch (start us, length us, event | category | flops | bytes accessed | tf_op | source)
XLA Modules:
  0.0 218.3 jit_solution(7277922570175208137)
XLA Ops:
  0.6 1.3 collective-permute-start
  1.9 3.3 %collective-permute-start.1 = (f32[2,256,256]{2,1,0:T(8,128)}, f32[2,256,256]{2,1,0:T(8,128)S(1)}, u32[]{:S(2)}, u32[]{:S(2)}) collective-permute-start(f32[2,256,256]{2,1,0:T(8,128)} %own_ref.1), channel_id=1, source_target_pairs={{4,0},{5,1},{6,2},{7,3},{8,4},{9,5},{10,6},{11,7},{12,8},{13,9},{1... | collective-permute-start | bytes 1572872 | tf_op jit(solution)/shard_map/ppermute | solution.py:421
  5.2 10.9 %collective-permute-done.right_ref = f32[2,256,256]{2,1,0:T(8,128)S(1)} collective-permute-done((f32[2,256,256]{2,1,0:T(8,128)}, f32[2,256,256]{2,1,0:T(8,128)S(1)}, u32[]{:S(2)}, u32[]{:S(2)}) %collective-permute-start) | collective-permute-done | bytes 524320 | tf_op jit(solution)/shard_map/ppermute | solution.py:420
  16.2 3.5 %collective-permute-start.2 = (f32[2,256,256]{2,1,0:T(8,128)S(1)}, f32[2,256,256]{2,1,0:T(8,128)S(1)}, u32[]{:S(2)}, u32[]{:S(2)}) collective-permute-start(f32[2,256,256]{2,1,0:T(8,128)S(1)} %collective-permute-done.right_ref), channel_id=1, source_target_pairs={{4,0},{5,1},{6,2},{7,3},{8,4},{9,5},{10,6},{11,7},{12,8},{13,9},{1... | collective-permute-start | bytes 1572872 | tf_op jit(solution)/shard_map/ppermute | solution.py:422
  20.3 1.8 multiply_convert_fusion
  22.0 0.0 collective-permute-done.1.below_ref
  22.1 5.7 %collective-permute-done.2.corner_ref = f32[2,256,256]{2,1,0:T(8,128)S(1)} collective-permute-done((f32[2,256,256]{2,1,0:T(8,128)S(1)}, f32[2,256,256]{2,1,0:T(8,128)S(1)}, u32[]{:S(2)}, u32[]{:S(2)}) %collective-permute-start.2) | collective-permute-done | bytes 524320 | tf_op jit(solution)/shard_map/ppermute | solution.py:422
  27.8 0.8 copy-done.17
  28.6 10.4 %frames.2 = (f32[64,4,8,128]{3,2,1,0:T(8,128)}, f32[64,4,8,128]{3,2,1,0:T(8,128)}, f32[2,2,256,256]{3,2,1,0:T(8,128)}, f32[3,256,256]{2,1,0:T(8,128)}, f32[3,256...) custom-call(s32[1]{0:T(128)} %bitcast.core_ref, s32[2,2]{1,0:T(2,128)} %pos_ref.3, ...), custom_call_target="tpu_custom_call" | custom-call | tf_op jit(solution)/shard_map/frames/pallas_call | solution.py:246
  39.0 0.1 collective-permute-start.6
  39.1 3.5 %collective-permute-start.3 = (f32[3,256,256]{2,1,0:T(8,128)}, f32[3,256,256]{2,1,0:T(8,128)}, u32[]{:S(2)}, u32[]{:S(2)}) collective-permute-start(f32[3,256,256]{2,1,0:T(8,128)} %get-tuple-element.27), channel_id=1, source_target_pairs={{0,4},{1,5},{2,6},{3,7},{4,8},{5,9},{6,10},{7,11},{8,12},{9,13},{1... | collective-permute-start | bytes 2359304 | tf_op jit(solution)/shard_map/ppermute | solution.py:431
  42.6 0.0 collective-permute-done.6
  42.6 2.5 %add.52 = f32[64,4,8,128]{3,2,1,0:T(8,128)} add(f32[64,4,8,128]{3,2,1,0:T(8,128)} %get-tuple-element.29, f32[64,4,8,128]{3,2,1,0:T(8,128)S(1)} %collective-permute-done.6) | non-fusion elementwise | flops 262144 | bytes 3145728 | tf_op jit(solution)/shard_map/add | solution.py:433
  45.1 11.9 %all-to-all-start = ((f32[64,4,8,128]{3,2,1,0:T(8,128)}), f32[64,4,8,128]{3,2,1,0:T(8,128)S(1)}, u32[]{:S(2)}, u32[]{:S(2)}) async-start(f32[64,4,8,128]{3,2,1,0:T(8,128)} %add.52), calls=%async_computation | async-start | bytes 2097152 | tf_op jit(solution)/shard_map/all_to_all | solution.py:436
  57.0 2.9 %collective-permute-start.5 = (f32[3,256,256]{2,1,0:T(8,128)}, f32[3,256,256]{2,1,0:T(8,128)S(1)}, u32[]{:S(2)}, u32[]{:S(2)}) collective-permute-start(f32[3,256,256]{2,1,0:T(8,128)} %get-tuple-element.28), channel_id=1, source_target_pairs={{0,4},{1,5},{2,6},{3,7},{4,8},{5,9},{6,10},{7,11},{8,12},{9,13},{1... | collective-permute-start | bytes 2359304 | tf_op jit(solution)/shard_map/ppermute | solution.py:435
  59.8 0.0 collective-permute-done.3
  59.9 2.1 add.47
  62.0 4.0 %collective-permute-start.4 = (f32[3,256,256]{2,1,0:T(8,128)}, f32[3,256,256]{2,1,0:T(8,128)}, u32[]{:S(2)}, u32[]{:S(2)}) collective-permute-start(f32[3,256,256]{2,1,0:T(8,128)} %add.47), channel_id=1, source_target_pairs={{0,1},{1,2},{2,3},{4,5},{5,6},{6,7},{8,9},{9,10},{10,11},{12,13},{... | collective-permute-start | bytes 2359304 | tf_op jit(solution)/shard_map/ppermute | solution.py:434
  66.0 9.5 %all-to-all-done.got_ref = f32[64,4,8,128]{3,2,1,0:T(8,128)S(1)} async-done(((f32[64,4,8,128]{3,2,1,0:T(8,128)}), f32[64,4,8,128]{3,2,1,0:T(8,128)S(1)}, u32[]{:S(2)}, u32[]{:S(2)}) %all-to-all-start) | async-done | bytes 1048608 | tf_op jit(solution)/shard_map/all_to_all | solution.py:436
  75.6 1.0 copy-done.4
  76.5 2.4 %spread.2 = f32[64,4,8,128]{3,2,1,0:T(8,128)} custom-call(f32[64,4,8,128]{3,2,1,0:T(8,128)} %copy-done.4), custom_call_target="tpu_custom_call" | custom-call | tf_op jit(solution)/shard_map/spread/pallas_call | solution.py:275
  79.0 4.8 %all-to-all-start.1 = ((f32[64,4,8,128]{3,2,1,0:T(8,128)}), f32[64,4,8,128]{3,2,1,0:T(8,128)S(1)}, u32[]{:S(2)}, u32[]{:S(2)}) async-start(f32[64,4,8,128]{3,2,1,0:T(8,128)} %spread.2), calls=%async_computation.1 | async-start | bytes 2097152 | tf_op jit(solution)/shard_map/all_to_all | solution.py:442
  83.8 0.0 copy-start.6
  83.8 0.0 collective-permute-done.5
  83.8 0.0 copy-start.12
  83.8 2.4 %collective-permute-done.4 = f32[3,256,256]{2,1,0:T(8,128)} collective-permute-done((f32[3,256,256]{2,1,0:T(8,128)}, f32[3,256,256]{2,1,0:T(8,128)}, u32[]{:S(2)}, u32[]{:S(2)}) %collective-permute-start.4) | collective-permute-done | bytes 786464 | tf_op jit(solution)/shard_map/ppermute | solution.py:434
  86.2 1.8 add_add_fusion.1
  88.0 13.6 %all-to-all-done.1.mine_ref = f32[64,4,8,128]{3,2,1,0:T(8,128)S(1)} async-done(((f32[64,4,8,128]{3,2,1,0:T(8,128)}), f32[64,4,8,128]{3,2,1,0:T(8,128)S(1)}, u32[]{:S(2)}, u32[]{:S(2)}) %all-to-all-start.1) | async-done | bytes 1048608 | tf_op jit(solution)/shard_map/all_to_all | solution.py:442
  101.6 1.9 collective-permute-start.7
  103.5 0.1 fusion.1.own_ref
  103.6 0.0 copy-start
  103.6 1.3 collective-permute-start.8
  104.9 1.9 collective-permute-start.9
  106.8 12.1 %collective-permute-done.8.right_ref = f32[2,256,256]{2,1,0:T(8,128)S(1)} collective-permute-done((f32[2,256,256]{2,1,0:T(8,128)S(1)}, f32[2,256,256]{2,1,0:T(8,128)S(1)}, u32[]{:S(2)}, u32[]{:S(2)}) %collective-permute-start.8) | collective-permute-done | bytes 524320 | tf_op jit(solution)/shard_map/ppermute | solution.py:420
  119.0 2.8 %collective-permute-start.10 = (f32[2,256,256]{2,1,0:T(8,128)S(1)}, f32[2,256,256]{2,1,0:T(8,128)S(1)}, u32[]{:S(2)}, u32[]{:S(2)}) collective-permute-start(f32[2,256,256]{2,1,0:T(8,128)S(1)} %collective-permute-done.8.right_ref), channel_id=1, source_target_pairs={{4,0},{5,1},{6,2},{7,3},{8,4},{9,5},{10,6},{11,7},{12,8},{13,9},{1... | collective-permute-start | bytes 1572872 | tf_op jit(solution)/shard_map/ppermute | solution.py:422
  121.7 0.0 collective-permute-done.7.other_ref
  121.7 1.0 copy-done.8
  122.7 6.7 %modes.2 = (f32[4,2,256,256]{3,2,1,0:T(8,128)}, f32[2,4]{1,0:T(2,128)}) custom-call(s32[1]{0:T(128)} %bitcast.core_ref, s32[1]{0:T(128)S(6)} %copy.9.cnt_ref, f32[2,4]{1,0:T(2,128)} %coef_ref.3, f32[64,4,8,128]{3,2,1,0:T(8,128)} %copy-done.3, f32[64,4,8,128]{3,2,1,0:T(8,128)} %copy-done.8, f32[4,2,256,256]{3,2,1,0:T(8,128)} %old_ref.1, ...), custom_call_target="tpu_custom_call" | custom-call | tf_op jit(solution)/shard_map/modes/pallas_call | solution.py:389
  129.4 0.0 collective-permute-done.9.below_ref
  129.5 0.0 collective-permute-done.10.corner_ref
  129.5 0.8 copy-done.16
  130.3 0.2 copy-done.18
  130.5 10.4 %frames.3 = (f32[64,4,8,128]{3,2,1,0:T(8,128)}, f32[64,4,8,128]{3,2,1,0:T(8,128)}, f32[2,2,256,256]{3,2,1,0:T(8,128)}, f32[3,256,256]{2,1,0:T(8,128)}, f32[3,256...) custom-call(s32[1]{0:T(128)} %bitcast.core_ref, s32[2,2]{1,0:T(2,128)} %pos_ref.3, ...), custom_call_target="tpu_custom_call" | custom-call | tf_op jit(solution)/shard_map/frames/pallas_call | solution.py:246
  140.9 0.1 collective-permute-start.14
  141.0 2.9 %collective-permute-done.14 = f32[64,4,8,128]{3,2,1,0:T(8,128)S(1)} collective-permute-done((f32[64,4,8,128]{3,2,1,0:T(8,128)}, f32[64,4,8,128]{3,2,1,0:T(8,128)S(1)}, u32[]{:S(2)}, u32[]{:S(2)}) %collective-permute-start.14) | collective-permute-done | bytes 1048608 | tf_op jit(solution)/shard_map/ppermute | solution.py:433
  143.8 2.4 %add.58 = f32[64,4,8,128]{3,2,1,0:T(8,128)} add(f32[64,4,8,128]{3,2,1,0:T(8,128)} %get-tuple-element.38, f32[64,4,8,128]{3,2,1,0:T(8,128)S(1)} %collective-permute-done.14) | non-fusion elementwise | flops 262144 | bytes 3145728 | tf_op jit(solution)/shard_map/add | solution.py:433
  146.2 6.3 %all-to-all-start.2 = ((f32[64,4,8,128]{3,2,1,0:T(8,128)}), f32[64,4,8,128]{3,2,1,0:T(8,128)S(1)}, u32[]{:S(2)}, u32[]{:S(2)}) async-start(f32[64,4,8,128]{3,2,1,0:T(8,128)} %add.58), calls=%async_computation.2 | async-start | bytes 2097152 | tf_op jit(solution)/shard_map/all_to_all | solution.py:436
  152.6 3.6 %collective-permute-start.11 = (f32[3,256,256]{2,1,0:T(8,128)}, f32[3,256,256]{2,1,0:T(8,128)S(1)}, u32[]{:S(2)}, u32[]{:S(2)}) collective-permute-start(f32[3,256,256]{2,1,0:T(8,128)} %get-tuple-element.36), channel_id=1, source_target_pairs={{0,4},{1,5},{2,6},{3,7},{4,8},{5,9},{6,10},{7,11},{8,12},{9,13},{1... | collective-permute-start | bytes 2359304 | tf_op jit(solution)/shard_map/ppermute | solution.py:431
  156.2 14.2 %all-to-all-done.2.got_ref = f32[64,4,8,128]{3,2,1,0:T(8,128)S(1)} async-done(((f32[64,4,8,128]{3,2,1,0:T(8,128)}), f32[64,4,8,128]{3,2,1,0:T(8,128)S(1)}, u32[]{:S(2)}, u32[]{:S(2)}) %all-to-all-start.2) | async-done | bytes 1048608 | tf_op jit(solution)/shard_map/all_to_all | solution.py:436
  170.5 1.0 copy-done.5
  171.5 2.4 %spread.3 = f32[64,4,8,128]{3,2,1,0:T(8,128)} custom-call(f32[64,4,8,128]{3,2,1,0:T(8,128)} %copy-done.5), custom_call_target="tpu_custom_call" | custom-call | tf_op jit(solution)/shard_map/spread/pallas_call | solution.py:275
  173.9 5.0 %all-to-all-start.3 = ((f32[64,4,8,128]{3,2,1,0:T(8,128)}), f32[64,4,8,128]{3,2,1,0:T(8,128)S(1)}, u32[]{:S(2)}, u32[]{:S(2)}) async-start(f32[64,4,8,128]{3,2,1,0:T(8,128)} %spread.3), calls=%async_computation.3 | async-start | bytes 2097152 | tf_op jit(solution)/shard_map/all_to_all | solution.py:442
  178.9 5.1 %collective-permute-start.13 = (f32[3,256,256]{2,1,0:T(8,128)}, f32[3,256,256]{2,1,0:T(8,128)}, u32[]{:S(2)}, u32[]{:S(2)}) collective-permute-start(f32[3,256,256]{2,1,0:T(8,128)} %get-tuple-element.37), channel_id=1, source_target_pairs={{0,4},{1,5},{2,6},{3,7},{4,8},{5,9},{6,10},{7,11},{8,12},{9,13},{1... | collective-permute-start | bytes 2359304 | tf_op jit(solution)/shard_map/ppermute | solution.py:435
  184.0 0.0 collective-permute-done.11
  184.1 1.0 add.53
  185.0 4.1 %collective-permute-start.12 = (f32[3,256,256]{2,1,0:T(8,128)}, f32[3,256,256]{2,1,0:T(8,128)}, u32[]{:S(2)}, u32[]{:S(2)}) collective-permute-start(f32[3,256,256]{2,1,0:T(8,128)} %add.53), channel_id=1, source_target_pairs={{0,1},{1,2},{2,3},{4,5},{5,6},{6,7},{8,9},{9,10},{10,11},{12,13},{... | collective-permute-start | bytes 2359304 | tf_op jit(solution)/shard_map/ppermute | solution.py:434
  189.2 6.0 %all-to-all-done.3.mine_ref = f32[64,4,8,128]{3,2,1,0:T(8,128)S(1)} async-done(((f32[64,4,8,128]{3,2,1,0:T(8,128)}), f32[64,4,8,128]{3,2,1,0:T(8,128)S(1)}, u32[]{:S(2)}, u32[]{:S(2)}) %all-to-all-start.3) | async-done | bytes 1048608 | tf_op jit(solution)/shard_map/all_to_all | solution.py:442
  195.2 5.7 %collective-permute-start.15 = (f32[64,4,8,128]{3,2,1,0:T(8,128)S(1)}, f32[64,4,8,128]{3,2,1,0:T(8,128)S(1)}, u32[]{:S(2)}, u32[]{:S(2)}) collective-permute-start(f32[64,4,8,128]{3,2,1,0:T(8,128)S(1)} %all-to-all-done.3.mine_ref), channel_id=1, source_target_pairs={{0,4},{4,0},{1,5},{5,1},{2,6},{6,2},{3,7},{7,3},{8,12},{12,8},{9,1... | collective-permute-start | bytes 3145736 | tf_op jit(solution)/shard_map/ppermute | solution.py:443
  200.8 0.0 collective-permute-done.13
  200.8 7.3 %collective-permute-done.12 = f32[3,256,256]{2,1,0:T(8,128)} collective-permute-done((f32[3,256,256]{2,1,0:T(8,128)}, f32[3,256,256]{2,1,0:T(8,128)}, u32[]{:S(2)}, u32[]{:S(2)}) %collective-permute-start.12) | collective-permute-done | bytes 786464 | tf_op jit(solution)/shard_map/ppermute | solution.py:434
  208.2 1.5 add_add_fusion
  209.7 0.9 fusion
  210.6 1.0 copy-done.7
  211.6 6.7 %modes.3 = (f32[4,2,256,256]{3,2,1,0:T(8,128)}, f32[2,4]{1,0:T(2,128)}) custom-call(s32[1]{0:T(128)} %bitcast.core_ref, s32[1]{0:T(128)S(6)} %copy.9.cnt_ref, f32[2,4]{1,0:T(2,128)} %get-tuple-element.32.coef_ref, f32[64,4,8,128]{3,2,1,0:T(8,128)} %copy-done.2, f32[64,4,8,128]{3,2,1,0:T(8,128)} %copy-done.7, ...), custom_call_target="tpu_custom_call" | custom-call | tf_op jit(solution)/shard_map/modes/pallas_call | solution.py:389
  (31 shorter events, 0.1 us)
Async XLA Ops:
  0.6 15.5 %collective-permute-start = (f32[2,256,256]{2,1,0:T(8,128)}, f32[2,256,256]{2,1,0:T(8,128)S(1)}, u32[]{:S(2)}, u32[]{:S(2)}) collective-permute-start(f32[2,256,256]{2,1,0:T(8,128)} %own_ref.1), channel_id=1, source_target_pairs={{1,0},{2,1},{3,2},{5,4},{6,5},{7,6},{9,8},{10,9},{11,10},{13,12},{... | collective-permute-start | bytes 1572872 | tf_op jit(solution)/shard_map/ppermute | solution.py:420
  1.9 20.1 %collective-permute-start.1 = (f32[2,256,256]{2,1,0:T(8,128)}, f32[2,256,256]{2,1,0:T(8,128)S(1)}, u32[]{:S(2)}, u32[]{:S(2)}) collective-permute-start(f32[2,256,256]{2,1,0:T(8,128)} %own_ref.1), channel_id=1, source_target_pairs={{4,0},{5,1},{6,2},{7,3},{8,4},{9,5},{10,6},{11,7},{12,8},{13,9},{1... | collective-permute-start | bytes 1572872 | tf_op jit(solution)/shard_map/ppermute | solution.py:421
  16.2 11.6 %copy-start.13 = (f32[2,256,256]{2,1,0:T(8,128)}, f32[2,256,256]{2,1,0:T(8,128)S(1)}, u32[]{:S(2)}) copy-start(f32[2,256,256]{2,1,0:T(8,128)S(1)} %collective-permute-done.right_ref) | copy-start | bytes 1572868
  16.2 11.6 %collective-permute-start.2 = (f32[2,256,256]{2,1,0:T(8,128)S(1)}, f32[2,256,256]{2,1,0:T(8,128)S(1)}, u32[]{:S(2)}, u32[]{:S(2)}) collective-permute-start(f32[2,256,256]{2,1,0:T(8,128)S(1)} %collective-permute-done.right_ref), channel_id=1, source_target_pairs={{4,0},{5,1},{6,2},{7,3},{8,4},{9,5},{10,6},{11,7},{12,8},{13,9},{1... | collective-permute-start | bytes 1572872 | tf_op jit(solution)/shard_map/ppermute | solution.py:422
  22.1 5.7 %copy-start.15 = (f32[2,256,256]{2,1,0:T(8,128)}, f32[2,256,256]{2,1,0:T(8,128)S(1)}, u32[]{:S(2)}) copy-start(f32[2,256,256]{2,1,0:T(8,128)S(1)} %collective-permute-done.1.below_ref) | copy-start | bytes 1572868
  27.7 0.8 copy-start.17
  39.0 3.6 %collective-permute-start.6 = (f32[64,4,8,128]{3,2,1,0:T(8,128)}, f32[64,4,8,128]{3,2,1,0:T(8,128)S(1)}, u32[]{:S(2)}, u32[]{:S(2)}) collective-permute-start(f32[64,4,8,128]{3,2,1,0:T(8,128)} %get-tuple-element.30), channel_id=1, source_target_pairs={{0,4},{4,0},{1,5},{5,1},{2,6},{6,2},{3,7},{7,3},{8,12},{12,8},{9,1... | collective-permute-start | bytes 3145736 | tf_op jit(solution)/shard_map/ppermute | solution.py:433
  39.1 20.8 %collective-permute-start.3 = (f32[3,256,256]{2,1,0:T(8,128)}, f32[3,256,256]{2,1,0:T(8,128)}, u32[]{:S(2)}, u32[]{:S(2)}) collective-permute-start(f32[3,256,256]{2,1,0:T(8,128)} %get-tuple-element.27), channel_id=1, source_target_pairs={{0,4},{1,5},{2,6},{3,7},{4,8},{5,9},{6,10},{7,11},{8,12},{9,13},{1... | collective-permute-start | bytes 2359304 | tf_op jit(solution)/shard_map/ppermute | solution.py:431
  42.6 17.3 %copy-start.11 = (f32[3,256,256]{2,1,0:T(8,128)S(1)}, f32[3,256,256]{2,1,0:T(8,128)}, u32[]{:S(2)}) copy-start(f32[3,256,256]{2,1,0:T(8,128)} %get-tuple-element.26) | copy-start | bytes 2359300
  45.1 30.5 %all-to-all-start = ((f32[64,4,8,128]{3,2,1,0:T(8,128)}), f32[64,4,8,128]{3,2,1,0:T(8,128)S(1)}, u32[]{:S(2)}, u32[]{:S(2)}) async-start(f32[64,4,8,128]{3,2,1,0:T(8,128)} %add.52), calls=%async_computation | async-start | bytes 2097152 | tf_op jit(solution)/shard_map/all_to_all | solution.py:436
  57.0 26.9 %collective-permute-start.5 = (f32[3,256,256]{2,1,0:T(8,128)}, f32[3,256,256]{2,1,0:T(8,128)S(1)}, u32[]{:S(2)}, u32[]{:S(2)}) collective-permute-start(f32[3,256,256]{2,1,0:T(8,128)} %get-tuple-element.28), channel_id=1, source_target_pairs={{0,4},{1,5},{2,6},{3,7},{4,8},{5,9},{6,10},{7,11},{8,12},{9,13},{1... | collective-permute-start | bytes 2359304 | tf_op jit(solution)/shard_map/ppermute | solution.py:435
  62.0 24.2 %collective-permute-start.4 = (f32[3,256,256]{2,1,0:T(8,128)}, f32[3,256,256]{2,1,0:T(8,128)}, u32[]{:S(2)}, u32[]{:S(2)}) collective-permute-start(f32[3,256,256]{2,1,0:T(8,128)} %add.47), channel_id=1, source_target_pairs={{0,1},{1,2},{2,3},{4,5},{5,6},{6,7},{8,9},{9,10},{10,11},{12,13},{... | collective-permute-start | bytes 2359304 | tf_op jit(solution)/shard_map/ppermute | solution.py:434
  75.6 1.0 copy-start.4
  79.0 22.7 %all-to-all-start.1 = ((f32[64,4,8,128]{3,2,1,0:T(8,128)}), f32[64,4,8,128]{3,2,1,0:T(8,128)S(1)}, u32[]{:S(2)}, u32[]{:S(2)}) async-start(f32[64,4,8,128]{3,2,1,0:T(8,128)} %spread.2), calls=%async_computation.1 | async-start | bytes 2097152 | tf_op jit(solution)/shard_map/all_to_all | solution.py:442
  83.8 19.7 %copy-start.6 = (f32[2,256,256]{2,1,0:T(8,128)S(1)}, f32[2,256,256]{2,1,0:T(8,128)}, u32[]{:S(2)}) copy-start(f32[2,256,256]{2,1,0:T(8,128)} %own_ref.1) | copy-start | bytes 1572868
  83.8 2.4 %copy-start.12 = (f32[3,256,256]{2,1,0:T(8,128)}, f32[3,256,256]{2,1,0:T(8,128)S(1)}, u32[]{:S(2)}) copy-start(f32[3,256,256]{2,1,0:T(8,128)S(1)} %collective-permute-done.5) | copy-start | bytes 2359300
  101.6 21.1 %copy-start.3 = (f32[64,4,8,128]{3,2,1,0:T(8,128)}, f32[64,4,8,128]{3,2,1,0:T(8,128)S(1)}, u32[]{:S(2)}) copy-start(f32[64,4,8,128]{3,2,1,0:T(8,128)S(1)} %all-to-all-done.1.mine_ref) | copy-start | bytes 3145732
  101.6 20.1 %collective-permute-start.7 = (f32[64,4,8,128]{3,2,1,0:T(8,128)S(1)}, f32[64,4,8,128]{3,2,1,0:T(8,128)S(1)}, u32[]{:S(2)}, u32[]{:S(2)}) collective-permute-start(f32[64,4,8,128]{3,2,1,0:T(8,128)S(1)} %all-to-all-done.1.mine_ref), channel_id=1, source_target_pairs={{0,4},{4,0},{1,5},{5,1},{2,6},{6,2},{3,7},{7,3},{8,12},{12,8},{9,1... | collective-permute-start | bytes 3145736 | tf_op jit(solution)/shard_map/ppermute | solution.py:443
  103.6 25.9 %copy-start = (f32[2,256,256]{2,1,0:T(8,128)}, f32[2,256,256]{2,1,0:T(8,128)S(1)}, u32[]{:S(2)}) copy-start(f32[2,256,256]{2,1,0:T(8,128)S(1)} %fusion.1.own_ref) | copy-start | bytes 1572868
  103.6 15.4 %collective-permute-start.8 = (f32[2,256,256]{2,1,0:T(8,128)S(1)}, f32[2,256,256]{2,1,0:T(8,128)S(1)}, u32[]{:S(2)}, u32[]{:S(2)}) collective-permute-start(f32[2,256,256]{2,1,0:T(8,128)S(1)} %fusion.1.own_ref), channel_id=1, source_target_pairs={{1,0},{2,1},{3,2},{5,4},{6,5},{7,6},{9,8},{10,9},{11,10},{13,12},{... | collective-permute-start | bytes 1572872 | tf_op jit(solution)/shard_map/ppermute | solution.py:420
  104.9 24.6 %collective-permute-start.9 = (f32[2,256,256]{2,1,0:T(8,128)S(1)}, f32[2,256,256]{2,1,0:T(8,128)S(1)}, u32[]{:S(2)}, u32[]{:S(2)}) collective-permute-start(f32[2,256,256]{2,1,0:T(8,128)S(1)} %fusion.1.own_ref), channel_id=1, source_target_pairs={{4,0},{5,1},{6,2},{7,3},{8,4},{9,5},{10,6},{11,7},{12,8},{13,9},{1... | collective-permute-start | bytes 1572872 | tf_op jit(solution)/shard_map/ppermute | solution.py:421
  119.0 10.5 %copy-start.14 = (f32[2,256,256]{2,1,0:T(8,128)}, f32[2,256,256]{2,1,0:T(8,128)S(1)}, u32[]{:S(2)}) copy-start(f32[2,256,256]{2,1,0:T(8,128)S(1)} %collective-permute-done.8.right_ref) | copy-start | bytes 1572868
  119.0 10.5 %collective-permute-start.10 = (f32[2,256,256]{2,1,0:T(8,128)S(1)}, f32[2,256,256]{2,1,0:T(8,128)S(1)}, u32[]{:S(2)}, u32[]{:S(2)}) collective-permute-start(f32[2,256,256]{2,1,0:T(8,128)S(1)} %collective-permute-done.8.right_ref), channel_id=1, source_target_pairs={{4,0},{5,1},{6,2},{7,3},{8,4},{9,5},{10,6},{11,7},{12,8},{13,9},{1... | collective-permute-start | bytes 1572872 | tf_op jit(solution)/shard_map/ppermute | solution.py:422
  121.7 1.0 copy-start.8
  129.5 0.8 copy-start.16
  129.5 1.0 copy-start.18
  140.9 3.0 %collective-permute-start.14 = (f32[64,4,8,128]{3,2,1,0:T(8,128)}, f32[64,4,8,128]{3,2,1,0:T(8,128)S(1)}, u32[]{:S(2)}, u32[]{:S(2)}) collective-permute-start(f32[64,4,8,128]{3,2,1,0:T(8,128)} %get-tuple-element.39), channel_id=1, source_target_pairs={{0,4},{4,0},{1,5},{5,1},{2,6},{6,2},{3,7},{7,3},{8,12},{12,8},{9,1... | collective-permute-start | bytes 3145736 | tf_op jit(solution)/shard_map/ppermute | solution.py:433
  146.2 24.2 %all-to-all-start.2 = ((f32[64,4,8,128]{3,2,1,0:T(8,128)}), f32[64,4,8,128]{3,2,1,0:T(8,128)S(1)}, u32[]{:S(2)}, u32[]{:S(2)}) async-start(f32[64,4,8,128]{3,2,1,0:T(8,128)} %add.58), calls=%async_computation.2 | async-start | bytes 2097152 | tf_op jit(solution)/shard_map/all_to_all | solution.py:436
  152.6 31.5 %copy-start.10 = (f32[3,256,256]{2,1,0:T(8,128)S(1)}, f32[3,256,256]{2,1,0:T(8,128)}, u32[]{:S(2)}) copy-start(f32[3,256,256]{2,1,0:T(8,128)} %get-tuple-element.35) | copy-start | bytes 2359300
  152.6 31.4 %collective-permute-start.11 = (f32[3,256,256]{2,1,0:T(8,128)}, f32[3,256,256]{2,1,0:T(8,128)S(1)}, u32[]{:S(2)}, u32[]{:S(2)}) collective-permute-start(f32[3,256,256]{2,1,0:T(8,128)} %get-tuple-element.36), channel_id=1, source_target_pairs={{0,4},{1,5},{2,6},{3,7},{4,8},{5,9},{6,10},{7,11},{8,12},{9,13},{1... | collective-permute-start | bytes 2359304 | tf_op jit(solution)/shard_map/ppermute | solution.py:431
  170.5 1.0 copy-start.5
  173.9 34.3 %copy-start.9 = (f32[3,256,256]{2,1,0:T(8,128)S(1)}, f32[3,256,256]{2,1,0:T(8,128)}, u32[]{:S(2)}) copy-start(f32[3,256,256]{2,1,0:T(8,128)} %get-tuple-element.34) | copy-start | bytes 2359300
  173.9 21.3 %all-to-all-start.3 = ((f32[64,4,8,128]{3,2,1,0:T(8,128)}), f32[64,4,8,128]{3,2,1,0:T(8,128)S(1)}, u32[]{:S(2)}, u32[]{:S(2)}) async-start(f32[64,4,8,128]{3,2,1,0:T(8,128)} %spread.3), calls=%async_computation.3 | async-start | bytes 2097152 | tf_op jit(solution)/shard_map/all_to_all | solution.py:442
  178.9 21.9 %collective-permute-start.13 = (f32[3,256,256]{2,1,0:T(8,128)}, f32[3,256,256]{2,1,0:T(8,128)}, u32[]{:S(2)}, u32[]{:S(2)}) collective-permute-start(f32[3,256,256]{2,1,0:T(8,128)} %get-tuple-element.37), channel_id=1, source_target_pairs={{0,4},{1,5},{2,6},{3,7},{4,8},{5,9},{6,10},{7,11},{8,12},{9,13},{1... | collective-permute-start | bytes 2359304 | tf_op jit(solution)/shard_map/ppermute | solution.py:435
  185.0 24.7 %copy-start.1 = (f32[2,256,256]{2,1,0:T(8,128)S(1)}, f32[2,256,256]{2,1,0:T(8,128)}, u32[]{:S(2)}) copy-start(f32[2,256,256]{2,1,0:T(8,128)} %copy-done) | copy-start | bytes 1572868
  185.0 23.1 %collective-permute-start.12 = (f32[3,256,256]{2,1,0:T(8,128)}, f32[3,256,256]{2,1,0:T(8,128)}, u32[]{:S(2)}, u32[]{:S(2)}) collective-permute-start(f32[3,256,256]{2,1,0:T(8,128)} %add.53), channel_id=1, source_target_pairs={{0,1},{1,2},{2,3},{4,5},{5,6},{6,7},{8,9},{9,10},{10,11},{12,13},{... | collective-permute-start | bytes 2359304 | tf_op jit(solution)/shard_map/ppermute | solution.py:434
  195.2 15.4 %copy-start.2 = (f32[64,4,8,128]{3,2,1,0:T(8,128)}, f32[64,4,8,128]{3,2,1,0:T(8,128)S(1)}, u32[]{:S(2)}) copy-start(f32[64,4,8,128]{3,2,1,0:T(8,128)S(1)} %all-to-all-done.3.mine_ref) | copy-start | bytes 3145732
  195.2 15.4 %collective-permute-start.15 = (f32[64,4,8,128]{3,2,1,0:T(8,128)S(1)}, f32[64,4,8,128]{3,2,1,0:T(8,128)S(1)}, u32[]{:S(2)}, u32[]{:S(2)}) collective-permute-start(f32[64,4,8,128]{3,2,1,0:T(8,128)S(1)} %all-to-all-done.3.mine_ref), channel_id=1, source_target_pairs={{0,4},{4,0},{1,5},{5,1},{2,6},{6,2},{3,7},{7,3},{8,12},{12,8},{9,1... | collective-permute-start | bytes 3145736 | tf_op jit(solution)/shard_map/ppermute | solution.py:443
  210.6 1.0 copy-start.7

commit v3 on v2

--- a/solution.py
+++ b/solution.py
@@ -17,6 +17,8 @@
 SCAN = ("z", "x", "core")
 ALL = ("z", "x", "core", "y")
 ROWS = 32
+CHUNKS = 4
+SMALL = pltpu.CompilerParams(vmem_limit_bytes=32 * 1024 * 1024)
 
 
 def make_tables(length):
@@ -43,15 +45,29 @@
     cols_ref[n:, n:] = cosine
 
 
+def near(x):
+    return pltpu.with_memory_space_constraint(x, pltpu.VMEM)
+
+
+def far(x):
+    return pltpu.with_memory_space_constraint(x, pltpu.HBM)
+
+
 def frames_kernel(
     core_ref, pos_ref, cnt_ref, coef_ref, own_ref, right_ref, below_ref, corner_ref,
-    amp_ref, modes_ref, cos_ref, sin_ref,
-    keep_ref, give_ref, grads_ref, t_own_ref, t_right_ref, t_below_ref, t_corner_ref,
+    amp_hbm, modes_in, cos_ref, sin_ref,
+    keep_ref, give_ref, grads_hbm, t_own_ref, t_right_ref, t_below_ref, t_corner_ref,
     ext_ref, tot_ref, probe_ref, exit_ref, rows_ref, cols_ref, stack_ref, side_ref, wide_ref,
-    in_sem, out_sem,
+    amp_ref, grads_ref, modes_ref, in_sem, out_sem, side_sem, *, staged,
 ):
     frames, n = amp_ref.shape[0], amp_ref.shape[1]
-    modes = modes_ref.shape[0]
+    modes = modes_in.shape[0]
+    amp_load = pltpu.make_async_copy(amp_hbm, amp_ref, side_sem.at[0])
+    modes_load = pltpu.make_async_copy(modes_in, modes_ref, side_sem.at[1])
+    if staged:
+        modes_load.start()
+    else:
+        modes_ref = modes_in
     lanes = n // 128
     is_first = core_ref[0] == 0
 
@@ -71,6 +87,7 @@
     loads += load(2, below_ref, n, 0) + load(3, corner_ref, n, lanes)
     for copy in loads:
         copy.start()
+    amp_load.start()
     fill_tables(cos_ref, sin_ref, rows_ref, cols_ref)
 
     def clear(t, carry):
@@ -91,6 +108,8 @@
     column = lax.broadcasted_iota(jnp.int32, (ROWS, 128), 1)
     for copy in loads:
         copy.wait()
+    if staged:
+        modes_load.wait()
 
     def patch_rows(f, plane, b):
         r, tile, shift = offsets[f]
@@ -142,6 +161,7 @@
             wide_ref[cols, :] = jnp.dot(side_ref[cols, :], second_ref[...], preferred_element_type=F32)
 
     transform(rows_ref, cols_ref)
+    amp_load.wait()
 
     def scale(b, carry):
         at = pl.ds(pl.multiple_of(b * ROWS, ROWS), ROWS)
@@ -229,25 +249,33 @@
                     give_ref[tile, k] = give[8 * i : 8 * i + 8]
         return carry
 
-    lax.fori_loop(0, n // 16, finish, 0)
+    for half in range(2):
+        lax.fori_loop(half * (n // 32), (half + 1) * (n // 32), finish, 0)
+        at = pl.ds(half * (n // 2), n // 2)
+        store = pltpu.make_async_copy(
+            grads_ref.at[:, :, at, :], grads_hbm.at[:, :, at, :], side_sem.at[2 + half]
+        )
+        store.start()
+        stores.append(store)
     for store in stores:
         store.wait()
 
 
-def run_frames(core, positions, count, coefficients, blocks, amplitudes, modes, tables):
+def run_frames(core, positions, count, coefficients, blocks, amplitudes, modes, tables, staged):
     frames, n = amplitudes.shape[0], amplitudes.shape[1]
     k = modes.shape[0]
     tiles = n * n // 1024
     smem = pl.BlockSpec(memory_space=pltpu.SMEM)
     vmem = pl.BlockSpec(memory_space=pltpu.VMEM)
     hbm = pl.BlockSpec(memory_space=pl.ANY)
-    piece = jax.ShapeDtypeStruct((tiles, k, 8, 128), F32)
-    quarter = jax.ShapeDtypeStruct((3, n, n), F32)
+    piece = pltpu.VMEM((tiles, k, 8, 128), F32)
+    quarter = pltpu.HBM((3, n, n), F32)
     return pl.pallas_call(
-        frames_kernel,
-        out_shape=(piece, piece, jax.ShapeDtypeStruct((frames, 2, n, n), F32)) + (quarter,) * 4,
-        in_specs=[smem] * 4 + [hbm] * 4 + [vmem] * 4,
-        out_specs=(vmem,) * 3 + (hbm,) * 4,
+        functools.partial(frames_kernel, staged=staged),
+        out_shape=(piece, piece, pltpu.HBM((frames, 2, n, n), F32)) + (quarter,) * 4,
+        in_specs=[smem] * 4 + [hbm] + [vmem] * 3 + [hbm, hbm if staged else vmem] + [vmem] * 2,
+        out_specs=(vmem,) * 2 + (hbm,) * 5,
+        compiler_params=SMALL,
         scratch_shapes=[
             pltpu.VMEM((2, 2 * n // 128, 2 * n, 128), F32),
             pltpu.VMEM((3, 2 * n // 128, 2 * n, 128), F32),
@@ -258,11 +286,19 @@
             pltpu.VMEM((2 * n, frames * n), BF16),
             pltpu.VMEM((frames * n, 2 * n), BF16),
             pltpu.VMEM((frames * n, 2 * n), F32),
+            pltpu.VMEM((frames, n, n), BF16),
+            pltpu.VMEM((frames, 2, n, n), F32),
+            pltpu.VMEM(modes.shape if staged else (8, 128), F32),
             pltpu.SemaphoreType.DMA((4 * n // 128,)),
             pltpu.SemaphoreType.DMA((4 * n // 128,)),
+            pltpu.SemaphoreType.DMA((4,)),
         ],
         name="frames",
-    )(core, positions, count, coefficients, *blocks, amplitudes, modes, *tables)
+    )(
+        core, far(positions), count, far(coefficients) if staged else coefficients,
+        far(blocks[0]) if staged else blocks[0], *map(near, blocks[1:]),
+        far(amplitudes), far(modes) if staged else near(modes), *tables,
+    )
 
 
 def spread_kernel(got_ref, out_ref):
@@ -274,9 +310,10 @@
     vmem = pl.BlockSpec(memory_space=pltpu.VMEM)
     return pl.pallas_call(
         spread_kernel,
-        out_shape=jax.ShapeDtypeStruct(got.shape, F32),
+        out_shape=pltpu.VMEM(got.shape, F32),
         in_specs=[vmem],
         out_specs=vmem,
+        compiler_params=SMALL,
         name="spread",
     )(got)
 
@@ -287,9 +324,20 @@
 
 
 def modes_kernel(
-    core_ref, cnt_ref, coef_ref, mine_ref, other_ref, old_ref, grads_ref, new_ref, out_coef_ref, raised_ref,
-    *, root_total,
+    core_ref, cnt_ref, coef_ref, mine_hbm, other_ref, old_hbm, grads_hbm, new_ref, out_coef_ref,
+    raised_ref, old_ref, grads_ref, mine_ref, sem, *, root_total,
 ):
+    part = old_ref.shape[2] // CHUNKS
+    tiles = mine_ref.shape[0] // CHUNKS
+    loads = []
+    for i in range(CHUNKS):
+        at = pl.ds(i * part, part)
+        loads.append(pltpu.make_async_copy(old_hbm.at[:, :, at, :], old_ref.at[:, :, at, :], sem.at[i]))
+        at = pl.ds(i * tiles, tiles)
+        loads.append(pltpu.make_async_copy(mine_hbm.at[at], mine_ref.at[at], sem.at[CHUNKS + 1 + i]))
+    grads_load = pltpu.make_async_copy(grads_hbm, grads_ref, sem.at[CHUNKS])
+    for load in loads + [grads_load]:
+        load.start()
     modes, n = old_ref.shape[0], old_ref.shape[2]
     frames = grads_ref.shape[0]
     pixels = n * n
@@ -321,7 +369,12 @@
                 acc[modes + 2 * p + 1] = acc[modes + 2 * p + 1] + (re[i] * im[j] - im[i] * re[j])
         return tuple(acc)
 
-    acc = lax.fori_loop(0, n // 8, lift, (zero,) * (modes + 2 * len(pairs)))
+    acc = (zero,) * (modes + 2 * len(pairs))
+    for i in range(CHUNKS):
+        loads[2 * i].wait()
+        loads[2 * i + 1].wait()
+        acc = lax.fori_loop(i * (part // 8), (i + 1) * (part // 8), lift, acc)
+    grads_load.wait()
     gram = [total_of(a) * (1.0 / pixels) for a in acc]
     upper = {}
     inverse = []
@@ -386,17 +439,25 @@
 def run_modes(core, count, coefficients, mine, other, old, grads, root_total):
     smem = pl.BlockSpec(memory_space=pltpu.SMEM)
     vmem = pl.BlockSpec(memory_space=pltpu.VMEM)
+    hbm = pl.BlockSpec(memory_space=pl.ANY)
     return pl.pallas_call(
         functools.partial(modes_kernel, root_total=root_total),
         out_shape=(
             jax.ShapeDtypeStruct(old.shape, F32),
             jax.ShapeDtypeStruct(coefficients.shape, F32),
         ),
-        in_specs=[smem] * 3 + [vmem] * 4,
+        in_specs=[smem] * 3 + [hbm, vmem] + [hbm] * 2,
         out_specs=(vmem, smem),
-        scratch_shapes=[pltpu.VMEM(old.shape, F32)],
+        scratch_shapes=[
+            pltpu.VMEM(old.shape, F32),
+            pltpu.VMEM(old.shape, F32),
+            pltpu.VMEM(grads.shape, F32),
+            pltpu.VMEM(mine.shape, F32),
+            pltpu.SemaphoreType.DMA((2 * CHUNKS + 1,)),
+        ],
+        compiler_params=SMALL,
         name="modes",
-    )(core, count, coefficients, mine, other, old, grads)
+    )(core, count, coefficients, far(mine), near(other), far(old), far(grads))
 
 
 def moves(scans, cols, down, over):
@@ -426,7 +487,8 @@
     blocks = widen(object_field)
     for iteration in range(ITERS):
         keep, give, grads, t_own, t_right, t_below, t_corner = run_frames(
-            core, positions, frame_count, coefficients, blocks, amplitudes, probe_modes, tables
+            core, positions, frame_count, coefficients, blocks, amplitudes, probe_modes, tables,
+            iteration == 0,
         )
         crossed = lax.ppermute(t_corner, ALL, moves(scans, cols, 1, 0))
         joined = t_right + crossed
@@ -438,7 +500,7 @@
         object_field = object_field + settled[:2] / (settled[2] + 1.0)
         if iteration + 1 < ITERS:
             blocks = widen(object_field)
-        spread = run_spread(got)
+        spread = run_spread(near(got))
         mine = lax.all_to_all(spread, CHIPS, split_axis=0, concat_axis=0, tiled=True)
         other = lax.ppermute(mine, "core", swap)
         probe_modes, coefficients = run_modes(

time: 220 us -> 205 us (0.932)
  Pallas kernels: 39 us -> 29.1 us
  waiting for transfers between devices: 84.7 us -> 91 us
  local copies, waits for them, and re-layouts: 5.8 us -> 0.04 us
  starting transfers between devices: 73.1 us -> 70.7 us
  other arithmetic: 14 us -> 11.7 us
    pallas_call x4, Pallas kernels: 25.6 us -> 17.6 us  [the longest x2 15.3 us: run_frames(): pl.pallas_call(functools.partial(frames_kernel, staged=staged), out_shape...]
    unnamed x38 -> x18, local copies, waits for them, and re-layouts: 5.8 us -> 0.04 us
    ppermute x2, waiting for transfers between devices: 9.7 us -> 15.4 us  [on_device(): arrived = lax.ppermute(joined, ALL, moves(scans, cols, 0, 1))]
    ppermute x2, waiting for transfers between devices: 5.7 us -> 8.43 us  [widen(): corner = lax.ppermute(right, ALL, moves(scans, cols, -1, 0))]
    add x2, other arithmetic: 4.88 us -> 2.36 us  [on_device(): kept = keep + lax.ppermute(give, 'core', swap)]
    all_to_all x2, waiting for transfers between devices: 19.6 us -> 17.1 us  [on_device(): lax.all_to_all(spread, CHIPS, split_axis=0, concat_axis=0, tiled=True)]
  transfers between devices with their start and end apart: 20 -> 20, of which waited for: 10 -> 11; matrix products, arithmetic and copies ran while one was open for 5% -> 5% of each run, Pallas kernels for 5% -> 4%
where the time goes in v3:
time: 205 us; the launch traced here: 204 us
  waiting for transfers between devices  91 us (44%)
  starting transfers between devices  70.7 us (34%)
  Pallas kernels  29.1 us (14%)
  other arithmetic  11.7 us (6%)
    all_to_all x2, waiting for transfers between devices, on_device(): got = lax.all_to_all(kept, CHIPS, split_axis=0, concat_axis=0, tiled=True)  24.5 us
    ppermute x2, waiting for transfers between devices, widen(): right = lax.ppermute(block, ALL, moves(scans, cols, 0, -1))  22.9 us
    all_to_all x2, starting transfers between devices, on_device(): got = lax.all_to_all(kept, CHIPS, split_axis=0, concat_axis=0, tiled=True)  18.4 us
    all_to_all x2, waiting for transfers between devices, on_device(): lax.all_to_all(spread, CHIPS, split_axis=0, concat_axis=0, tiled=True)  17.1 us
    ppermute x2, waiting for transfers between devices, on_device(): arrived = lax.ppermute(joined, ALL, moves(scans, cols, 0, 1))  15.4 us
    pallas_call x2, Pallas kernels, run_frames(): pl.pallas_call(functools.partial(frames_kernel, staged=staged), out_shape...  15.3 us
    pallas_call x2, Pallas kernels, run_modes(): pl.pallas_call(functools.partial(modes_kernel, root_total=root_total), ou...  11.5 us
    all_to_all x2, starting transfers between devices, on_device(): lax.all_to_all(spread, CHIPS, split_axis=0, concat_axis=0, tiled=True)  9.77 us
  transfers between devices with their start and end apart: 20, of which 11 were waited for; matrix products, arithmetic and copies ran while one was open for 5% of the time, Pallas kernels for 4%

profile of v3, /device:TPU:1, one launch (start us, length us, event | category | flops | bytes accessed | tf_op | source)
XLA Modules:
  0.0 204.2 jit_solution(11449575068309796259)
XLA Ops:
  0.6 1.3 collective-permute-start
  1.9 3.3 %collective-permute-start.1 = (f32[2,256,256]{2,1,0:T(8,128)}, f32[2,256,256]{2,1,0:T(8,128)S(1)}, u32[]{:S(2)}, u32[]{:S(2)}) collective-permute-start(f32[2,256,256]{2,1,0:T(8,128)} %own_ref.1), channel_id=1, source_target_pairs={{4,0},{5,1},{6,2},{7,3},{8,4},{9,5},{10,6},{11,7},{12,8},{13,9},{1... | collective-permute-start | bytes 1572872 | tf_op jit(solution)/shard_map/ppermute | solution.py:482
  5.2 10.9 %collective-permute-done.right_ref = f32[2,256,256]{2,1,0:T(8,128)S(1)} collective-permute-done((f32[2,256,256]{2,1,0:T(8,128)}, f32[2,256,256]{2,1,0:T(8,128)S(1)}, u32[]{:S(2)}, u32[]{:S(2)}) %collective-permute-start) | collective-permute-done | bytes 524320 | tf_op jit(solution)/shard_map/ppermute | solution.py:481
  16.2 3.5 %collective-permute-start.2 = (f32[2,256,256]{2,1,0:T(8,128)S(1)}, f32[2,256,256]{2,1,0:T(8,128)S(1)}, u32[]{:S(2)}, u32[]{:S(2)}) collective-permute-start(f32[2,256,256]{2,1,0:T(8,128)S(1)} %collective-permute-done.right_ref), channel_id=1, source_target_pairs={{4,0},{5,1},{6,2},{7,3},{8,4},{9,5},{10,6},{11,7},{12,8},{13,9},{1... | collective-permute-start | bytes 1572872 | tf_op jit(solution)/shard_map/ppermute | solution.py:483
  20.3 1.1 multiply_convert_fusion
  21.4 0.0 collective-permute-done.1.below_ref
  21.4 6.3 %collective-permute-done.2.corner_ref = f32[2,256,256]{2,1,0:T(8,128)S(1)} collective-permute-done((f32[2,256,256]{2,1,0:T(8,128)S(1)}, f32[2,256,256]{2,1,0:T(8,128)S(1)}, u32[]{:S(2)}, u32[]{:S(2)}) %collective-permute-start.2) | collective-permute-done | bytes 524320 | tf_op jit(solution)/shard_map/ppermute | solution.py:483
  27.7 8.3 %frames.2 = (f32[64,4,8,128]{3,2,1,0:T(8,128)S(1)}, f32[64,4,8,128]{3,2,1,0:T(8,128)S(1)}, f32[2,2,256,256]{3,2,1,0:T(8,128)}, f32[3,256,256]{2,1,0:T(8,128)}, f...) custom-call(s32[1]{0:T(128)} %bitcast.core_ref, s32[2,2]{1,0:T(2,128)} %pos_ref.3, ...), custom_call_target="tpu_custom_call" | custom-call | tf_op jit(solution)/shard_map/frames/pallas_call | solution.py:273
  36.0 0.1 collective-permute-start.6
  36.1 3.5 %collective-permute-start.3 = (f32[3,256,256]{2,1,0:T(8,128)}, f32[3,256,256]{2,1,0:T(8,128)}, u32[]{:S(2)}, u32[]{:S(2)}) collective-permute-start(f32[3,256,256]{2,1,0:T(8,128)} %get-tuple-element.27), channel_id=1, source_target_pairs={{0,4},{1,5},{2,6},{3,7},{4,8},{5,9},{6,10},{7,11},{8,12},{9,13},{1... | collective-permute-start | bytes 2359304 | tf_op jit(solution)/shard_map/ppermute | solution.py:493
  39.6 0.0 collective-permute-done.6
  39.6 0.0 copy-start.7
  39.6 1.2 add.52
  40.8 11.9 %all-to-all-start = ((f32[64,4,8,128]{3,2,1,0:T(8,128)}), f32[64,4,8,128]{3,2,1,0:T(8,128)S(1)}, u32[]{:S(2)}, u32[]{:S(2)}) async-start(f32[64,4,8,128]{3,2,1,0:T(8,128)} %add.52), calls=%async_computation | async-start | bytes 2097152 | tf_op jit(solution)/shard_map/all_to_all | solution.py:498
  52.7 2.7 %collective-permute-start.5 = (f32[3,256,256]{2,1,0:T(8,128)}, f32[3,256,256]{2,1,0:T(8,128)S(1)}, u32[]{:S(2)}, u32[]{:S(2)}) collective-permute-start(f32[3,256,256]{2,1,0:T(8,128)} %get-tuple-element.28), channel_id=1, source_target_pairs={{0,4},{1,5},{2,6},{3,7},{4,8},{5,9},{6,10},{7,11},{8,12},{9,13},{1... | collective-permute-start | bytes 2359304 | tf_op jit(solution)/shard_map/ppermute | solution.py:497
  55.4 0.0 collective-permute-done.3
  55.4 0.0 copy-done.7
  55.4 2.1 %add.47 = f32[3,256,256]{2,1,0:T(8,128)} add(f32[3,256,256]{2,1,0:T(8,128)S(1)} %copy-done.7, f32[3,256,256]{2,1,0:T(8,128)} %collective-permute-done.3) | non-fusion elementwise | flops 196608 | bytes 2359296 | tf_op jit(solution)/shard_map/add | solution.py:494
  57.5 4.0 %collective-permute-start.4 = (f32[3,256,256]{2,1,0:T(8,128)}, f32[3,256,256]{2,1,0:T(8,128)}, u32[]{:S(2)}, u32[]{:S(2)}) collective-permute-start(f32[3,256,256]{2,1,0:T(8,128)} %add.47), channel_id=1, source_target_pairs={{0,1},{1,2},{2,3},{4,5},{5,6},{6,7},{8,9},{9,10},{10,11},{12,13},{... | collective-permute-start | bytes 2359304 | tf_op jit(solution)/shard_map/ppermute | solution.py:496
  61.5 10.3 %all-to-all-done.got_ref = f32[64,4,8,128]{3,2,1,0:T(8,128)S(1)} async-done(((f32[64,4,8,128]{3,2,1,0:T(8,128)}), f32[64,4,8,128]{3,2,1,0:T(8,128)S(1)}, u32[]{:S(2)}, u32[]{:S(2)}) %all-to-all-start) | async-done | bytes 1048608 | tf_op jit(solution)/shard_map/all_to_all | solution.py:498
  71.8 1.2 spread.2
  72.9 4.7 %all-to-all-start.1 = ((f32[64,4,8,128]{3,2,1,0:T(8,128)}), f32[64,4,8,128]{3,2,1,0:T(8,128)S(1)}, u32[]{:S(2)}, u32[]{:S(2)}) async-start(f32[64,4,8,128]{3,2,1,0:T(8,128)} %spread.2), calls=%async_computation.1 | async-start | bytes 2097152 | tf_op jit(solution)/shard_map/all_to_all | solution.py:504
  77.7 0.0 copy-start.4
  77.7 0.0 collective-permute-done.5
  77.7 0.0 copy-start.8
  77.7 7.8 %collective-permute-done.4 = f32[3,256,256]{2,1,0:T(8,128)} collective-permute-done((f32[3,256,256]{2,1,0:T(8,128)}, f32[3,256,256]{2,1,0:T(8,128)}, u32[]{:S(2)}, u32[]{:S(2)}) %collective-permute-start.4) | collective-permute-done | bytes 786464 | tf_op jit(solution)/shard_map/ppermute | solution.py:496
  85.5 0.0 copy-done.8
  85.5 1.8 add_add_fusion.1
  87.3 11.3 %all-to-all-done.1.mine_hbm = f32[64,4,8,128]{3,2,1,0:T(8,128)S(1)} async-done(((f32[64,4,8,128]{3,2,1,0:T(8,128)}), f32[64,4,8,128]{3,2,1,0:T(8,128)S(1)}, u32[]{:S(2)}, u32[]{:S(2)}) %all-to-all-start.1) | async-done | bytes 1048608 | tf_op jit(solution)/shard_map/all_to_all | solution.py:504
  98.6 0.4 collective-permute-start.7
  99.0 0.0 copy-done.4
  99.0 0.1 fusion.1.own_ref
  99.1 1.3 collective-permute-start.8
  100.4 2.0 collective-permute-start.9
  102.4 11.9 %collective-permute-done.8.right_ref = f32[2,256,256]{2,1,0:T(8,128)S(1)} collective-permute-done((f32[2,256,256]{2,1,0:T(8,128)S(1)}, f32[2,256,256]{2,1,0:T(8,128)S(1)}, u32[]{:S(2)}, u32[]{:S(2)}) %collective-permute-start.8) | collective-permute-done | bytes 524320 | tf_op jit(solution)/shard_map/ppermute | solution.py:481
  114.4 2.9 %collective-permute-start.10 = (f32[2,256,256]{2,1,0:T(8,128)S(1)}, f32[2,256,256]{2,1,0:T(8,128)S(1)}, u32[]{:S(2)}, u32[]{:S(2)}) collective-permute-start(f32[2,256,256]{2,1,0:T(8,128)S(1)} %collective-permute-done.8.right_ref), channel_id=1, source_target_pairs={{4,0},{5,1},{6,2},{7,3},{8,4},{9,5},{10,6},{11,7},{12,8},{13,9},{1... | collective-permute-start | bytes 1572872 | tf_op jit(solution)/shard_map/ppermute | solution.py:483
  117.2 0.0 collective-permute-done.7.other_ref
  117.3 5.5 %modes.2 = (f32[4,2,256,256]{3,2,1,0:T(8,128)S(1)}, f32[2,4]{1,0:T(2,128)S(1)}) custom-call(s32[1]{0:T(128)} %bitcast.core_ref, s32[1]{0:T(128)S(6)} %copy.9.cnt_ref, f32[2,4]{1,0:T(2,128)S(1)} %copy-done.1, f32[64,4,8,128]{3,2,1,0:T(8,128)} %copy-done.3, f32[64,4,8,128]{3,2,1,0:T(8,128)S(1)} %collective-permute-done.7.other_ref, ...), custom_call_target="tpu_custom_call" | custom-call | tf_op jit(solution)/shard_map/modes/pallas_call | solution.py:443
  122.7 0.0 collective-permute-done.9.below_ref
  122.7 2.1 %collective-permute-done.10.corner_ref = f32[2,256,256]{2,1,0:T(8,128)S(1)} collective-permute-done((f32[2,256,256]{2,1,0:T(8,128)S(1)}, f32[2,256,256]{2,1,0:T(8,128)S(1)}, u32[]{:S(2)}, u32[]{:S(2)}) %collective-permute-start.10) | collective-permute-done | bytes 524320 | tf_op jit(solution)/shard_map/ppermute | solution.py:483
  124.9 7.0 %frames.3 = (f32[64,4,8,128]{3,2,1,0:T(8,128)S(1)}, f32[64,4,8,128]{3,2,1,0:T(8,128)S(1)}, f32[2,2,256,256]{3,2,1,0:T(8,128)}, f32[3,256,256]{2,1,0:T(8,128)}, f...) custom-call(s32[1]{0:T(128)} %bitcast.core_ref, s32[2,2]{1,0:T(2,128)} %pos_ref.3, ...), custom_call_target="tpu_custom_call" | custom-call | tf_op jit(solution)/shard_map/frames/pallas_call | solution.py:273
  131.9 0.1 collective-permute-start.14
  132.0 2.6 %collective-permute-done.14 = f32[64,4,8,128]{3,2,1,0:T(8,128)S(1)} collective-permute-done((f32[64,4,8,128]{3,2,1,0:T(8,128)S(1)}, f32[64,4,8,128]{3,2,1,0:T(8,128)S(1)}, u32[]{:S(2)}, u32[]{:S(2)}) %collective-permute-start.14) | collective-permute-done | bytes 1048608 | tf_op jit(solution)/shard_map/ppermute | solution.py:495
  134.7 1.2 add.58
  135.8 6.5 %all-to-all-start.2 = ((f32[64,4,8,128]{3,2,1,0:T(8,128)}), f32[64,4,8,128]{3,2,1,0:T(8,128)S(1)}, u32[]{:S(2)}, u32[]{:S(2)}) async-start(f32[64,4,8,128]{3,2,1,0:T(8,128)} %add.58), calls=%async_computation.2 | async-start | bytes 2097152 | tf_op jit(solution)/shard_map/all_to_all | solution.py:498
  142.3 3.6 %collective-permute-start.11 = (f32[3,256,256]{2,1,0:T(8,128)}, f32[3,256,256]{2,1,0:T(8,128)}, u32[]{:S(2)}, u32[]{:S(2)}) collective-permute-start(f32[3,256,256]{2,1,0:T(8,128)} %get-tuple-element.36), channel_id=1, source_target_pairs={{0,4},{1,5},{2,6},{3,7},{4,8},{5,9},{6,10},{7,11},{8,12},{9,13},{1... | collective-permute-start | bytes 2359304 | tf_op jit(solution)/shard_map/ppermute | solution.py:493
  146.0 14.2 %all-to-all-done.2.got_ref = f32[64,4,8,128]{3,2,1,0:T(8,128)S(1)} async-done(((f32[64,4,8,128]{3,2,1,0:T(8,128)}), f32[64,4,8,128]{3,2,1,0:T(8,128)S(1)}, u32[]{:S(2)}, u32[]{:S(2)}) %all-to-all-start.2) | async-done | bytes 1048608 | tf_op jit(solution)/shard_map/all_to_all | solution.py:498
  160.2 1.2 spread.3
  161.4 5.0 %all-to-all-start.3 = ((f32[64,4,8,128]{3,2,1,0:T(8,128)}), f32[64,4,8,128]{3,2,1,0:T(8,128)S(1)}, u32[]{:S(2)}, u32[]{:S(2)}) async-start(f32[64,4,8,128]{3,2,1,0:T(8,128)} %spread.3), calls=%async_computation.3 | async-start | bytes 2097152 | tf_op jit(solution)/shard_map/all_to_all | solution.py:504
  166.4 5.1 %collective-permute-start.13 = (f32[3,256,256]{2,1,0:T(8,128)}, f32[3,256,256]{2,1,0:T(8,128)}, u32[]{:S(2)}, u32[]{:S(2)}) collective-permute-start(f32[3,256,256]{2,1,0:T(8,128)} %get-tuple-element.37), channel_id=1, source_target_pairs={{0,4},{1,5},{2,6},{3,7},{4,8},{5,9},{6,10},{7,11},{8,12},{9,13},{1... | collective-permute-start | bytes 2359304 | tf_op jit(solution)/shard_map/ppermute | solution.py:497
  171.5 0.0 collective-permute-done.11
  171.6 0.0 copy-done.6
  171.6 2.1 %add.53 = f32[3,256,256]{2,1,0:T(8,128)} add(f32[3,256,256]{2,1,0:T(8,128)S(1)} %copy-done.6, f32[3,256,256]{2,1,0:T(8,128)} %collective-permute-done.11) | non-fusion elementwise | flops 196608 | bytes 2359296 | tf_op jit(solution)/shard_map/add | solution.py:494
  173.7 3.1 %collective-permute-start.12 = (f32[3,256,256]{2,1,0:T(8,128)}, f32[3,256,256]{2,1,0:T(8,128)S(1)}, u32[]{:S(2)}, u32[]{:S(2)}) collective-permute-start(f32[3,256,256]{2,1,0:T(8,128)} %add.53), channel_id=1, source_target_pairs={{0,1},{1,2},{2,3},{4,5},{5,6},{6,7},{8,9},{9,10},{10,11},{12,13},{... | collective-permute-start | bytes 2359304 | tf_op jit(solution)/shard_map/ppermute | solution.py:496
  176.8 5.8 %all-to-all-done.3.mine_hbm = f32[64,4,8,128]{3,2,1,0:T(8,128)S(1)} async-done(((f32[64,4,8,128]{3,2,1,0:T(8,128)}), f32[64,4,8,128]{3,2,1,0:T(8,128)S(1)}, u32[]{:S(2)}, u32[]{:S(2)}) %all-to-all-start.3) | async-done | bytes 1048608 | tf_op jit(solution)/shard_map/all_to_all | solution.py:504
  182.7 5.7 %collective-permute-start.15 = (f32[64,4,8,128]{3,2,1,0:T(8,128)S(1)}, f32[64,4,8,128]{3,2,1,0:T(8,128)S(1)}, u32[]{:S(2)}, u32[]{:S(2)}) collective-permute-start(f32[64,4,8,128]{3,2,1,0:T(8,128)S(1)} %all-to-all-done.3.mine_hbm), channel_id=1, source_target_pairs={{0,4},{4,0},{1,5},{5,1},{2,6},{6,2},{3,7},{7,3},{8,12},{12,8},{9,1... | collective-permute-start | bytes 3145736 | tf_op jit(solution)/shard_map/ppermute | solution.py:505
  188.3 0.0 collective-permute-done.13
  188.3 7.6 %collective-permute-done.12 = f32[3,256,256]{2,1,0:T(8,128)S(1)} collective-permute-done((f32[3,256,256]{2,1,0:T(8,128)}, f32[3,256,256]{2,1,0:T(8,128)S(1)}, u32[]{:S(2)}, u32[]{:S(2)}) %collective-permute-start.12) | collective-permute-done | bytes 786464 | tf_op jit(solution)/shard_map/ppermute | solution.py:496
  196.0 0.0 copy-done.5
  196.0 1.3 add_add_fusion
  197.3 0.9 fusion
  198.2 0.0 copy-done.2
  198.2 0.0 collective-permute-done.15.other_ref
  198.2 6.0 %modes.3 = (f32[4,2,256,256]{3,2,1,0:T(8,128)}, f32[2,4]{1,0:T(2,128)}) custom-call(s32[1]{0:T(128)} %bitcast.core_ref, s32[1]{0:T(128)S(6)} %copy.9.cnt_ref, f32[2,4]{1,0:T(2,128)S(1)} %get-tuple-element.32.coef_ref, f32[64,4,8,128]{3,2,1,0:T(8,128)} %copy-done.2, f32[64,4,8,128]{3,2,1,0:T(8,128)S(1)} %collective-permute-done.15.other_ref, ...), custom_call_target="tpu_custom_call" | custom-call | tf_op jit(solution)/shard_map/modes/pallas_call | solution.py:443
  (11 shorter events, 0.1 us)
Async XLA Ops:
  0.6 15.5 %collective-permute-start = (f32[2,256,256]{2,1,0:T(8,128)}, f32[2,256,256]{2,1,0:T(8,128)S(1)}, u32[]{:S(2)}, u32[]{:S(2)}) collective-permute-start(f32[2,256,256]{2,1,0:T(8,128)} %own_ref.1), channel_id=1, source_target_pairs={{1,0},{2,1},{3,2},{5,4},{6,5},{7,6},{9,8},{10,9},{11,10},{13,12},{... | collective-permute-start | bytes 1572872 | tf_op jit(solution)/shard_map/ppermute | solution.py:481
  1.9 19.5 %collective-permute-start.1 = (f32[2,256,256]{2,1,0:T(8,128)}, f32[2,256,256]{2,1,0:T(8,128)S(1)}, u32[]{:S(2)}, u32[]{:S(2)}) collective-permute-start(f32[2,256,256]{2,1,0:T(8,128)} %own_ref.1), channel_id=1, source_target_pairs={{4,0},{5,1},{6,2},{7,3},{8,4},{9,5},{10,6},{11,7},{12,8},{13,9},{1... | collective-permute-start | bytes 1572872 | tf_op jit(solution)/shard_map/ppermute | solution.py:482
  16.2 11.6 %collective-permute-start.2 = (f32[2,256,256]{2,1,0:T(8,128)S(1)}, f32[2,256,256]{2,1,0:T(8,128)S(1)}, u32[]{:S(2)}, u32[]{:S(2)}) collective-permute-start(f32[2,256,256]{2,1,0:T(8,128)S(1)} %collective-permute-done.right_ref), channel_id=1, source_target_pairs={{4,0},{5,1},{6,2},{7,3},{8,4},{9,5},{10,6},{11,7},{12,8},{13,9},{1... | collective-permute-start | bytes 1572872 | tf_op jit(solution)/shard_map/ppermute | solution.py:483
  36.0 3.6 %collective-permute-start.6 = (f32[64,4,8,128]{3,2,1,0:T(8,128)S(1)}, f32[64,4,8,128]{3,2,1,0:T(8,128)S(1)}, u32[]{:S(2)}, u32[]{:S(2)}) collective-permute-start(f32[64,4,8,128]{3,2,1,0:T(8,128)S(1)} %get-tuple-element.30), channel_id=1, source_target_pairs={{0,4},{4,0},{1,5},{5,1},{2,6},{6,2},{3,7},{7,3},{8,12},{12,8},{9,1... | collective-permute-start | bytes 3145736 | tf_op jit(solution)/shard_map/ppermute | solution.py:495
  36.1 19.3 %collective-permute-start.3 = (f32[3,256,256]{2,1,0:T(8,128)}, f32[3,256,256]{2,1,0:T(8,128)}, u32[]{:S(2)}, u32[]{:S(2)}) collective-permute-start(f32[3,256,256]{2,1,0:T(8,128)} %get-tuple-element.27), channel_id=1, source_target_pairs={{0,4},{1,5},{2,6},{3,7},{4,8},{5,9},{6,10},{7,11},{8,12},{9,13},{1... | collective-permute-start | bytes 2359304 | tf_op jit(solution)/shard_map/ppermute | solution.py:493
  39.6 15.8 %copy-start.7 = (f32[3,256,256]{2,1,0:T(8,128)S(1)}, f32[3,256,256]{2,1,0:T(8,128)}, u32[]{:S(2)}) copy-start(f32[3,256,256]{2,1,0:T(8,128)} %get-tuple-element.26) | copy-start | bytes 2359300
  40.8 31.0 %all-to-all-start = ((f32[64,4,8,128]{3,2,1,0:T(8,128)}), f32[64,4,8,128]{3,2,1,0:T(8,128)S(1)}, u32[]{:S(2)}, u32[]{:S(2)}) async-start(f32[64,4,8,128]{3,2,1,0:T(8,128)} %add.52), calls=%async_computation | async-start | bytes 2097152 | tf_op jit(solution)/shard_map/all_to_all | solution.py:498
  52.7 25.0 %collective-permute-start.5 = (f32[3,256,256]{2,1,0:T(8,128)}, f32[3,256,256]{2,1,0:T(8,128)S(1)}, u32[]{:S(2)}, u32[]{:S(2)}) collective-permute-start(f32[3,256,256]{2,1,0:T(8,128)} %get-tuple-element.28), channel_id=1, source_target_pairs={{0,4},{1,5},{2,6},{3,7},{4,8},{5,9},{6,10},{7,11},{8,12},{9,13},{1... | collective-permute-start | bytes 2359304 | tf_op jit(solution)/shard_map/ppermute | solution.py:497
  57.5 28.0 %collective-permute-start.4 = (f32[3,256,256]{2,1,0:T(8,128)}, f32[3,256,256]{2,1,0:T(8,128)}, u32[]{:S(2)}, u32[]{:S(2)}) collective-permute-start(f32[3,256,256]{2,1,0:T(8,128)} %add.47), channel_id=1, source_target_pairs={{0,1},{1,2},{2,3},{4,5},{5,6},{6,7},{8,9},{9,10},{10,11},{12,13},{... | collective-permute-start | bytes 2359304 | tf_op jit(solution)/shard_map/ppermute | solution.py:496
  72.9 25.7 %all-to-all-start.1 = ((f32[64,4,8,128]{3,2,1,0:T(8,128)}), f32[64,4,8,128]{3,2,1,0:T(8,128)S(1)}, u32[]{:S(2)}, u32[]{:S(2)}) async-start(f32[64,4,8,128]{3,2,1,0:T(8,128)} %spread.2), calls=%async_computation.1 | async-start | bytes 2097152 | tf_op jit(solution)/shard_map/all_to_all | solution.py:504
  77.7 21.3 %copy-start.4 = (f32[2,256,256]{2,1,0:T(8,128)S(1)}, f32[2,256,256]{2,1,0:T(8,128)}, u32[]{:S(2)}) copy-start(f32[2,256,256]{2,1,0:T(8,128)} %own_ref.1) | copy-start | bytes 1572868
  77.7 7.8 %copy-start.8 = (f32[3,256,256]{2,1,0:T(8,128)}, f32[3,256,256]{2,1,0:T(8,128)S(1)}, u32[]{:S(2)}) copy-start(f32[3,256,256]{2,1,0:T(8,128)S(1)} %collective-permute-done.5) | copy-start | bytes 2359300
  85.5 31.7 %copy-start.1 = (f32[2,4]{1,0:T(2,128)S(1)}, f32[2,4]{1,0:T(2,128)}, u32[]{:S(2)}) copy-start(f32[2,4]{1,0:T(2,128)} %coef_ref.3) | copy-start | bytes 100
  98.6 18.6 %copy-start.3 = (f32[64,4,8,128]{3,2,1,0:T(8,128)}, f32[64,4,8,128]{3,2,1,0:T(8,128)S(1)}, u32[]{:S(2)}) copy-start(f32[64,4,8,128]{3,2,1,0:T(8,128)S(1)} %all-to-all-done.1.mine_hbm) | copy-start | bytes 3145732
  98.6 18.6 %collective-permute-start.7 = (f32[64,4,8,128]{3,2,1,0:T(8,128)S(1)}, f32[64,4,8,128]{3,2,1,0:T(8,128)S(1)}, u32[]{:S(2)}, u32[]{:S(2)}) collective-permute-start(f32[64,4,8,128]{3,2,1,0:T(8,128)S(1)} %all-to-all-done.1.mine_hbm), channel_id=1, source_target_pairs={{0,4},{4,0},{1,5},{5,1},{2,6},{6,2},{3,7},{7,3},{8,12},{12,8},{9,1... | collective-permute-start | bytes 3145736 | tf_op jit(solution)/shard_map/ppermute | solution.py:505
  99.1 15.3 %collective-permute-start.8 = (f32[2,256,256]{2,1,0:T(8,128)S(1)}, f32[2,256,256]{2,1,0:T(8,128)S(1)}, u32[]{:S(2)}, u32[]{:S(2)}) collective-permute-start(f32[2,256,256]{2,1,0:T(8,128)S(1)} %fusion.1.own_ref), channel_id=1, source_target_pairs={{1,0},{2,1},{3,2},{5,4},{6,5},{7,6},{9,8},{10,9},{11,10},{13,12},{... | collective-permute-start | bytes 1572872 | tf_op jit(solution)/shard_map/ppermute | solution.py:481
  100.4 22.3 %collective-permute-start.9 = (f32[2,256,256]{2,1,0:T(8,128)S(1)}, f32[2,256,256]{2,1,0:T(8,128)S(1)}, u32[]{:S(2)}, u32[]{:S(2)}) collective-permute-start(f32[2,256,256]{2,1,0:T(8,128)S(1)} %fusion.1.own_ref), channel_id=1, source_target_pairs={{4,0},{5,1},{6,2},{7,3},{8,4},{9,5},{10,6},{11,7},{12,8},{13,9},{1... | collective-permute-start | bytes 1572872 | tf_op jit(solution)/shard_map/ppermute | solution.py:482
  114.4 10.5 %collective-permute-start.10 = (f32[2,256,256]{2,1,0:T(8,128)S(1)}, f32[2,256,256]{2,1,0:T(8,128)S(1)}, u32[]{:S(2)}, u32[]{:S(2)}) collective-permute-start(f32[2,256,256]{2,1,0:T(8,128)S(1)} %collective-permute-done.8.right_ref), channel_id=1, source_target_pairs={{4,0},{5,1},{6,2},{7,3},{8,4},{9,5},{10,6},{11,7},{12,8},{13,9},{1... | collective-permute-start | bytes 1572872 | tf_op jit(solution)/shard_map/ppermute | solution.py:483
  122.7 9.2 %copy-start = (f32[4,2,256,256]{3,2,1,0:T(8,128)}, f32[4,2,256,256]{3,2,1,0:T(8,128)S(1)}, u32[]{:S(2)}) copy-start(f32[4,2,256,256]{3,2,1,0:T(8,128)S(1)} %get-tuple-element.33.modes_in.old_hbm) | copy-start | bytes 6291460
  131.9 2.7 %collective-permute-start.14 = (f32[64,4,8,128]{3,2,1,0:T(8,128)S(1)}, f32[64,4,8,128]{3,2,1,0:T(8,128)S(1)}, u32[]{:S(2)}, u32[]{:S(2)}) collective-permute-start(f32[64,4,8,128]{3,2,1,0:T(8,128)S(1)} %get-tuple-element.39), channel_id=1, source_target_pairs={{0,4},{4,0},{1,5},{5,1},{2,6},{6,2},{3,7},{7,3},{8,12},{12,8},{9,1... | collective-permute-start | bytes 3145736 | tf_op jit(solution)/shard_map/ppermute | solution.py:495
  135.8 24.4 %all-to-all-start.2 = ((f32[64,4,8,128]{3,2,1,0:T(8,128)}), f32[64,4,8,128]{3,2,1,0:T(8,128)S(1)}, u32[]{:S(2)}, u32[]{:S(2)}) async-start(f32[64,4,8,128]{3,2,1,0:T(8,128)} %add.58), calls=%async_computation.2 | async-start | bytes 2097152 | tf_op jit(solution)/shard_map/all_to_all | solution.py:498
  142.3 29.3 %copy-start.6 = (f32[3,256,256]{2,1,0:T(8,128)S(1)}, f32[3,256,256]{2,1,0:T(8,128)}, u32[]{:S(2)}) copy-start(f32[3,256,256]{2,1,0:T(8,128)} %get-tuple-element.35) | copy-start | bytes 2359300
  142.3 29.2 %collective-permute-start.11 = (f32[3,256,256]{2,1,0:T(8,128)}, f32[3,256,256]{2,1,0:T(8,128)}, u32[]{:S(2)}, u32[]{:S(2)}) collective-permute-start(f32[3,256,256]{2,1,0:T(8,128)} %get-tuple-element.36), channel_id=1, source_target_pairs={{0,4},{1,5},{2,6},{3,7},{4,8},{5,9},{6,10},{7,11},{8,12},{9,13},{1... | collective-permute-start | bytes 2359304 | tf_op jit(solution)/shard_map/ppermute | solution.py:493
  161.4 34.6 %copy-start.5 = (f32[3,256,256]{2,1,0:T(8,128)S(1)}, f32[3,256,256]{2,1,0:T(8,128)}, u32[]{:S(2)}) copy-start(f32[3,256,256]{2,1,0:T(8,128)} %get-tuple-element.34) | copy-start | bytes 2359300
  161.4 21.3 %all-to-all-start.3 = ((f32[64,4,8,128]{3,2,1,0:T(8,128)}), f32[64,4,8,128]{3,2,1,0:T(8,128)S(1)}, u32[]{:S(2)}, u32[]{:S(2)}) async-start(f32[64,4,8,128]{3,2,1,0:T(8,128)} %spread.3), calls=%async_computation.3 | async-start | bytes 2097152 | tf_op jit(solution)/shard_map/all_to_all | solution.py:504
  166.4 21.9 %collective-permute-start.13 = (f32[3,256,256]{2,1,0:T(8,128)}, f32[3,256,256]{2,1,0:T(8,128)}, u32[]{:S(2)}, u32[]{:S(2)}) collective-permute-start(f32[3,256,256]{2,1,0:T(8,128)} %get-tuple-element.37), channel_id=1, source_target_pairs={{0,4},{1,5},{2,6},{3,7},{4,8},{5,9},{6,10},{7,11},{8,12},{9,13},{1... | collective-permute-start | bytes 2359304 | tf_op jit(solution)/shard_map/ppermute | solution.py:497
  173.7 22.3 %collective-permute-start.12 = (f32[3,256,256]{2,1,0:T(8,128)}, f32[3,256,256]{2,1,0:T(8,128)S(1)}, u32[]{:S(2)}, u32[]{:S(2)}) collective-permute-start(f32[3,256,256]{2,1,0:T(8,128)} %add.53), channel_id=1, source_target_pairs={{0,1},{1,2},{2,3},{4,5},{5,6},{6,7},{8,9},{9,10},{10,11},{12,13},{... | collective-permute-start | bytes 2359304 | tf_op jit(solution)/shard_map/ppermute | solution.py:496
  182.7 15.5 %copy-start.2 = (f32[64,4,8,128]{3,2,1,0:T(8,128)}, f32[64,4,8,128]{3,2,1,0:T(8,128)S(1)}, u32[]{:S(2)}) copy-start(f32[64,4,8,128]{3,2,1,0:T(8,128)S(1)} %all-to-all-done.3.mine_hbm) | copy-start | bytes 3145732
  182.7 15.5 %collective-permute-start.15 = (f32[64,4,8,128]{3,2,1,0:T(8,128)S(1)}, f32[64,4,8,128]{3,2,1,0:T(8,128)S(1)}, u32[]{:S(2)}, u32[]{:S(2)}) collective-permute-start(f32[64,4,8,128]{3,2,1,0:T(8,128)S(1)} %all-to-all-done.3.mine_hbm), channel_id=1, source_target_pairs={{0,4},{4,0},{1,5},{5,1},{2,6},{6,2},{3,7},{7,3},{8,12},{12,8},{9,1... | collective-permute-start | bytes 3145736 | tf_op jit(solution)/shard_map/ppermute | solution.py:505
